TPU v7x, 32 devices: a whole 2x2x4 slice. The times are simulated.
32 devices in a mesh: sp: 8 (over y, x, core), ch: 4 (over z).
Axes of the slice: x: 2, y: 2, z: 4, core: 2. Of those that a mesh axis runs over, the one named last changes fastest.
Arguments:
- features: bfloat16 [64, 64, 2, 2, 14, 128], P(None, ('sp', 'ch')), may hold values from -6 to 6
- pre_act: bfloat16 [128, 32, 14, 128], P(None, ('sp', 'ch')), may hold values from -6 to 6
- cotangent: bfloat16 [128, 32, 14, 128], P(None, ('sp', 'ch')), may hold values from -12 to 12
- weight: bfloat16 [27, 64, 128], replicated, may hold values from -0.15625 to 0.15625
Outputs:
- data_grad: bfloat16 [64, 64, 2, 2, 14, 128], P(None, ('sp', 'ch'))
- weight_grad: float32 [27, 64, 128], replicated
All inputs are finite; a program needn't handle non-finite values.
Results may differ from a plain program's by a relative error of at most 0.0025.
Values may be sent and summed in bfloat16 or wider, within the bound.
A program may use at most 64 MiB of HBM per device.

v0:
```python
import functools
import math

import jax
import jax.numpy as jnp
from jax import lax
from jax.experimental import pallas as pl
from jax.experimental.pallas import tpu as pltpu
from jax.sharding import PartitionSpec as P

MESH = pl.DeviceIdType.MESH
LANES = 128
UNIT = 8


def kernel(cfg, pre_hbm, cot_hbm, feat_hbm, w_hbm, dg_hbm, wg_hbm, *scr):
    (pre_v, cot_v, feat_v, w_v, m_nat, h_nat, mh, mn, feat_a, wl, wf, ws, dg_v, grad, out_v) = scr[:15]
    r1, r2, r3 = scr[15:18]
    in_sem, out_sem, halo_s, halo_r, sA, rA = scr[18:]
    chips, chs, rows, c_in, c_out, scale, chunks, taps_first = cfg
    sp = lax.axis_index("sp")
    ch = lax.axis_index("ch")
    chip = sp // 2
    core = sp % 2
    flat = sp * chs + ch
    last = chips * 2 * chs - 1
    span = rows * LANES

    loads = [
        pltpu.make_async_copy(pre_hbm.at[0], pre_v, in_sem.at[0]),
        pltpu.make_async_copy(cot_hbm.at[0], cot_v, in_sem.at[1]),
        pltpu.make_async_copy(w_hbm, w_v, in_sem.at[2]),
    ]
    for ld in loads:
        ld.start()

    def load_feat(k, carry):
        p, s, b = k // (2 * rows), (k // rows) % 2, k % rows
        pltpu.make_async_copy(feat_hbm.at[:, p, s, b], feat_v.at[p, s, b], in_sem.at[3]).start()
        return carry

    lax.fori_loop(0, 4 * rows, load_feat, 0)

    bar = pltpu.get_barrier_semaphore()
    pl.semaphore_signal(bar, inc=1, device_id=(sp + 1 - 2 * core, ch), device_id_type=MESH)
    for k in range(1, chips):
        pl.semaphore_signal(bar, inc=1, device_id=(((chip + k) % chips) * 2 + core, ch), device_id_type=MESH)
    for k in range(1, chs):
        pl.semaphore_signal(bar, inc=1, device_id=(sp, (ch + k) % chs), device_id_type=MESH)
    prev = jnp.maximum(flat - 1, 0)
    nxt = jnp.minimum(flat + 1, last)

    @pl.when(flat > 0)
    def _():
        pl.semaphore_signal(bar, inc=1, device_id=(prev // chs, prev % chs), device_id_type=MESH)

    @pl.when(flat < last)
    def _():
        pl.semaphore_signal(bar, inc=1, device_id=(nxt // chs, nxt % chs), device_id_type=MESH)

    loads[0].wait()
    loads[1].wait()

    def mask_step(b, carry):
        p = pre_v[b].astype(jnp.float32)
        m_nat[b] = jnp.where(p > 0, cot_v[b].astype(jnp.float32), 0.0).astype(jnp.bfloat16)
        return carry

    lax.fori_loop(0, rows, mask_step, 0)
    peers = chips + chs - 1 + jnp.minimum(flat, 1) + jnp.minimum(last - flat, 1)
    pl.semaphore_wait(bar, peers)

    halo = pltpu.make_async_remote_copy(
        src_ref=m_nat, dst_ref=h_nat, send_sem=halo_s, recv_sem=halo_r,
        device_id=(prev // chs, prev % chs), device_id_type=MESH,
    )

    @pl.when(flat > 0)
    def _():
        halo.start()

    lane = lax.broadcasted_iota(jnp.int32, (c_out, LANES), 1)

    def spread(src, dst):
        dst[:, span:] = jnp.zeros((2 * c_out, LANES), jnp.bfloat16)
        for b in range(rows):
            v = src[b]
            dst[:c_out, b * LANES:(b + 1) * LANES] = v
            r = jnp.where(lane == LANES - 1, 0.0, pltpu.roll(v.astype(jnp.float32), LANES - 1, 1))
            dst[c_out:, b * LANES:(b + 1) * LANES] = r.astype(jnp.bfloat16)

    spread(m_nat, mh)
    pltpu.make_async_copy(feat_v, feat_v, in_sem.at[3]).wait()
    two = 2 * c_in

    feat_rows = feat_v.reshape(2, 2, rows, two, LANES)

    def feat_step(k, carry):
        p, s = k // 2, k % 2
        at = pl.ds(pl.multiple_of(s * two, two), two)
        for b in range(rows):
            feat_a[p, at, b * LANES:(b + 1) * LANES] = feat_rows[p, s, b]
        return carry

    lax.fori_loop(0, 4, feat_step, 0)

    kd_slot = {1: 0, 2: 1, 0: 2}
    ups = c_in // UNIT

    def unit_of(order):
        if order < taps_first:
            return order * ups
        return chunks[1][0] + (order - taps_first) * ups

    def put(kd, kh, kw, val):
        base = unit_of(kd_slot[kd] * 9 + kh * 3 + kw)
        grad[base:base + ups] = val.reshape(ups, UNIT, c_out)

    def wgrad(kd, p, mm):
        dn = (((1,), (1,)), ((), ()))
        o = lax.dot_general(feat_a[p], mm[:, :span], dn, preferred_element_type=jnp.float32)
        d = lax.dot_general(feat_a[p, two:], mm[:, LANES:], dn, preferred_element_type=jnp.float32)
        for r in range(2):
            ws[r, :2 * two] = o[:, r * c_out:(r + 1) * c_out]
            ws[r, 2 * two:] = d[:, r * c_out:(r + 1) * c_out]
        for kh, part in ((1, 0), (2, 1), (0, 2)):
            for kw, r, t in ((1, 0, 0), (2, 0, 1), (0, 1, 1)):
                put(kd, kh, kw, ws[r, pl.ds(part * two + t, c_in, stride=2), :])

    def weights():
        def step(kd, carry):
            for part, kh in enumerate((1, 2, 0)):
                base = kd * 9 + kh * 3
                wf[0, pl.ds(0, c_in, stride=2), :] = w_v[base + 1].astype(jnp.float32)
                wf[0, pl.ds(1, c_in, stride=2), :] = w_v[base + 2].astype(jnp.float32)
                wf[1, pl.ds(0, c_in, stride=2), :] = jnp.zeros((c_in, c_out), jnp.float32)
                wf[1, pl.ds(1, c_in, stride=2), :] = w_v[base].astype(jnp.float32)
                for r in range(2):
                    wl[kd, part * two:(part + 1) * two, r * c_out:(r + 1) * c_out] = wf[r].astype(jnp.bfloat16)
            return carry

        lax.fori_loop(0, 3, step, 0)

    dg_rows = dg_v.reshape(2, 2, rows, two, LANES)

    def dgrad(p, terms):
        def step(k, carry):
            col = pl.multiple_of(k * 2 * LANES, 2 * LANES)
            here = pl.ds(col, 2 * LANES)
            down = pl.ds(pl.multiple_of(col + LANES, LANES), 2 * LANES)
            top, bot = None, None
            for kd, mm in terms:
                o = jnp.dot(wl[kd, :2 * two], mm[:, here], preferred_element_type=jnp.float32)
                d = jnp.dot(wl[kd, 2 * two:], mm[:, down], preferred_element_type=jnp.float32)
                top = o[:two] if top is None else top + o[:two]
                bot = o[two:] + d if bot is None else bot + (o[two:] + d)
            for s, val in ((0, top), (1, bot)):
                for j in range(2):
                    b = 2 * k + j
                    dg_rows[p, s, b] = val[:, j * LANES:(j + 1) * LANES].astype(jnp.bfloat16)
                    pltpu.make_async_copy(dg_v.at[p, s, b], dg_hbm.at[p, s, b], out_sem.at[p]).start()
            return carry

        lax.fori_loop(0, rows // 2, step, 0)

    class Reduce:
        def __init__(self, idx, base, u):
            self.i, self.base, self.u = idx, base, u
            self.zu = u * chs
            self.half = self.zu * chips
            self.copies = {}

        def remote(self, stage, k, src, dst, dev):
            sem = stage_base[stage] + k
            return pltpu.make_async_remote_copy(
                src_ref=src, dst_ref=dst, send_sem=sA.at[self.i, sem], recv_sem=rA.at[self.i, sem],
                device_id=dev, device_id_type=MESH)

        def chip_dev(self, k):
            return (((chip + k) % chips) * 2 + core, ch)

        def ch_dev(self, k):
            return (sp, (ch + k) % chs)

        def off(self, a, b, c):
            return self.base + (a * self.half) + b * self.zu + c * self.u

        def start(self, stage):
            cps = []
            other = (sp + 1 - 2 * core, ch)
            if stage == 1:
                cps.append(self.remote(1, 0, grad.at[pl.ds(self.off(1 - core, 0, 0), self.half)], r1.at[self.i, pl.ds(0, self.half)], other))
            elif stage == 2:
                for k in range(1, chips):
                    to = (chip + k) % chips
                    cps.append(self.remote(2, k - 1, grad.at[pl.ds(self.off(core, to, 0), self.zu)], r2.at[self.i, k - 1, pl.ds(0, self.zu)], self.chip_dev(k)))
            elif stage == 3:
                for k in range(1, chs):
                    to = (ch + k) % chs
                    cps.append(self.remote(3, k - 1, grad.at[pl.ds(self.off(core, chip, to), self.u)], r3.at[self.i, k - 1, pl.ds(0, self.u)], self.ch_dev(k)))
            elif stage == 4:
                ref = out_v.at[pl.ds(self.off(core, chip, ch), self.u)]
                for k in range(1, chs):
                    cps.append(self.remote(4, k - 1, ref, ref, self.ch_dev(k)))
            elif stage == 5:
                ref = out_v.at[pl.ds(self.off(core, chip, 0), self.zu)]
                for k in range(1, chips):
                    cps.append(self.remote(5, k - 1, ref, ref, self.chip_dev(k)))
            else:
                ref = out_v.at[pl.ds(self.off(core, 0, 0), self.half)]
                cps.append(self.remote(6, 0, ref, ref, other))
            for c in cps:
                c.start()
            self.copies[stage] = cps

        def finish(self, stage):
            for c in self.copies[stage]:
                c.wait_send()
                c.wait_recv()
            if stage == 1:
                s = pl.ds(self.off(core, 0, 0), self.half)
                grad[s] = grad[s] + r1[self.i, :self.half]
            elif stage == 2:
                s = pl.ds(self.off(core, chip, 0), self.zu)
                v = grad[s]
                for k in range(chips - 1):
                    v = v + r2[self.i, k, :self.zu]
                grad[s] = v
            elif stage == 3:
                s = pl.ds(self.off(core, chip, ch), self.u)
                v = grad[s]
                for k in range(chs - 1):
                    v = v + r3[self.i, k, :self.u]
                out_v[s] = v * scale

    stage_base = {1: 0, 2: 1, 3: chips, 4: chips + chs - 1, 5: chips + 2 * chs - 2, 6: 2 * chips + 2 * chs - 3}
    red_a = Reduce(0, *chunks[0])
    red_b = Reduce(1, *chunks[1])

    for lo, hi in ((taps_first * ups, chunks[1][0]), (unit_of(27), grad.shape[0])):
        if lo < hi:
            grad[lo:hi] = jnp.zeros((hi - lo, UNIT, LANES), jnp.float32)

    wgrad(1, 0, mh)
    wgrad(2, 1, mh)
    red_a.start(1)
    loads[2].wait()
    weights()
    dgrad(0, [(1, mh)])
    red_a.finish(1)
    red_a.start(2)

    @pl.when(flat > 0)
    def _():
        halo.wait_send()

    @pl.when(flat < last)
    def _():
        halo.wait_recv()

    @pl.when(flat == last)
    def _():
        h_nat[...] = jnp.zeros_like(h_nat)

    spread(h_nat, mn)
    wgrad(0, 1, mn)
    red_b.start(1)
    red_a.finish(2)
    red_a.start(3)
    dgrad(1, [(2, mh), (0, mn)])
    red_b.finish(1)
    red_b.start(2)
    red_a.finish(3)
    red_a.start(4)
    red_b.finish(2)
    red_b.start(3)
    red_a.finish(4)
    red_a.start(5)
    red_b.finish(3)
    red_b.start(4)
    red_a.finish(5)
    red_a.start(6)
    red_b.finish(4)
    red_b.start(5)
    red_a.finish(6)
    red_b.finish(5)
    red_b.start(6)
    red_b.finish(6)
    outs = []
    for k, (order, count, tap0) in enumerate(
        ((0, taps_first, 9), (taps_first, 18 - taps_first, 9 + taps_first), (18, 9, 0))
    ):
        outs.append(
            pltpu.make_async_copy(
                out_v.at[pl.ds(unit_of(order), count * ups)],
                wg_hbm.at[pl.ds(tap0 * ups, count * ups)],
                out_sem.at[2 + k],
            )
        )
        outs[-1].start()
    for p in range(2):
        pltpu.make_async_copy(dg_v.at[p], dg_v.at[p], out_sem.at[p]).wait()
    for out in outs:
        out.wait()


def store_kernel(dg_in, wg_in, dg_out, wg_out, sem):
    rows = dg_in.shape[2]
    wg_copy = pltpu.make_async_copy(wg_in, wg_out, sem.at[0])
    wg_copy.start()

    def step(k, carry):
        p, s, b = k // (2 * rows), (k // rows) % 2, k % rows
        pltpu.make_async_copy(dg_in.at[p, s, b], dg_out.at[:, p, s, b], sem.at[1]).start()
        return carry

    lax.fori_loop(0, 4 * rows, step, 0)
    pltpu.make_async_copy(dg_in, dg_in, sem.at[1]).wait()
    wg_copy.wait()


def on_device(features, pre_act, cotangent, weight):
    c_in, planes_in, _, _, rows, cols = features.shape
    c_out, planes = pre_act.shape[:2]
    taps = weight.shape[0]
    chips = lax.axis_size("sp") // 2
    chs = lax.axis_size("ch")
    devices = chips * 2 * chs
    scale = 1.0 / math.sqrt(devices * planes * rows * cols)
    ups = c_in // UNIT
    total = taps * ups
    taps_first = 16
    u_a = -(-(taps_first * ups) // devices)
    u_b = -(-(total - taps_first * ups) // devices)
    chunks = ((0, u_a), (u_a * devices, u_b))
    units = (u_a + u_b) * devices
    u_max = max(u_a, u_b)
    n_sems = 2 * chips + 2 * chs - 2
    cfg = (chips, chs, rows, c_in, c_out, scale, chunks, taps_first)
    bf, f32 = jnp.bfloat16, jnp.float32
    held = 2 * (units + u_max * chs * chips + chips * u_max * chs + chs * u_max)
    vmem = 17 * 2**20 + held * UNIT * c_out * 4
    span = rows * cols
    any_spec = pl.BlockSpec(memory_space=pl.ANY)
    dg, wg = pl.pallas_call(
        functools.partial(kernel, cfg),
        out_shape=(
            jax.ShapeDtypeStruct((2, 2, rows, c_in, 2, cols), bf),
            jax.ShapeDtypeStruct((total, UNIT, c_out), f32),
        ),
        in_specs=[pl.BlockSpec(memory_space=pltpu.HBM)] * 4,
        out_specs=(any_spec, any_spec),
        scratch_shapes=[
            pltpu.VMEM((rows, c_out, cols), bf),
            pltpu.VMEM((rows, c_out, cols), bf),
            pltpu.VMEM((2, 2, rows, c_in, 2, cols), bf),
            pltpu.VMEM(weight.shape, bf),
            pltpu.VMEM((rows, c_out, cols), bf),
            pltpu.VMEM((rows, c_out, cols), bf),
            pltpu.VMEM((2 * c_out, span + cols), bf),
            pltpu.VMEM((2 * c_out, span + cols), bf),
            pltpu.VMEM((2, 4 * c_in, span), bf),
            pltpu.VMEM((3, 6 * c_in, 2 * c_out), bf),
            pltpu.VMEM((2, 2 * c_in, c_out), f32),
            pltpu.VMEM((2, 6 * c_in, c_out), f32),
            pltpu.VMEM((2, 2, rows, c_in, 2, cols), bf),
            pltpu.VMEM((units, UNIT, c_out), f32),
            pltpu.VMEM((units, UNIT, c_out), f32),
            pltpu.VMEM((2, u_max * chs * chips, UNIT, c_out), f32),
            pltpu.VMEM((2, max(1, chips - 1), u_max * chs, UNIT, c_out), f32),
            pltpu.VMEM((2, max(1, chs - 1), u_max, UNIT, c_out), f32),
            pltpu.SemaphoreType.DMA((4,)),
            pltpu.SemaphoreType.DMA((5,)),
            pltpu.SemaphoreType.DMA,
            pltpu.SemaphoreType.DMA,
            pltpu.SemaphoreType.DMA((2, n_sems)),
            pltpu.SemaphoreType.DMA((2, n_sems)),
        ],
        compiler_params=pltpu.CompilerParams(
            collective_id=0, has_side_effects=True, vmem_limit_bytes=vmem
        ),
    )(
        pltpu.with_memory_space_constraint(pre_act.transpose(1, 2, 0, 3), pltpu.HBM),
        pltpu.with_memory_space_constraint(cotangent.transpose(1, 2, 0, 3), pltpu.HBM),
        pltpu.with_memory_space_constraint(features.transpose(0, 1, 2, 4, 3, 5), pltpu.HBM),
        pltpu.with_memory_space_constraint(weight, pltpu.HBM),
    )
    dg, wg = pl.pallas_call(
        store_kernel,
        out_shape=(
            jax.ShapeDtypeStruct((c_in, planes_in, 2, rows, 2, cols), bf),
            jax.ShapeDtypeStruct(wg.shape, f32),
        ),
        in_specs=[any_spec] * 2,
        out_specs=(pl.BlockSpec(memory_space=pltpu.HBM),) * 2,
        scratch_shapes=[pltpu.SemaphoreType.DMA((2,))],
        compiler_params=pltpu.CompilerParams(vmem_limit_bytes=2**20),
    )(dg, wg)
    return dg.transpose(0, 1, 2, 4, 3, 5), wg.reshape(taps, c_in, c_out)


def solution(mesh):
    return jax.shard_map(
        on_device,
        mesh=mesh,
        in_specs=(
            P(None, ("sp", "ch"), None, None, None, None),
            P(None, ("sp", "ch"), None, None),
            P(None, ("sp", "ch"), None, None),
            P(),
        ),
        out_specs=(P(None, ("sp", "ch"), None, None, None, None), P()),
        check_vma=False,
    )
```

profile of v0, /device:TPU:0, one launch (start us, length us, event | category | flops | bytes accessed | tf_op | source)
XLA Modules:
  0.0 42.8 jit_solution(2023254744530833720)
XLA Ops:
  0.6 40.3 %shard_map.59 = (bf16[2,2,14,64,2,128]{5,4,3,2,1,0:T(2,128)(2,1)S(1)}, f32[216,8,128]{2,1,0:T(8,128)S(1)}) custom-call(bf16[1,14,128,128]{3,2,1,0:T(8,128)(2,1)} %bitcast.6, bf16[1,14,128,128]{3,2,1,0:T(8,128)(2,1)} %bitcast.7, bf16[64,2,2,14,2,128]{5,4,3,2,1,0:T(2,128)(2,1)} %bitcast.5, bf16[27,64,128]{2,1,0:T(8,128)(2,1)} %w_hbm.1), custom_call_target="tpu_custom_call" | custom-call | tf_op jit(solution)/shard_map/pallas_call | solution.py:345
  41.0 1.8 %shard_map.60 = (bf16[64,2,2,14,2,128]{5,4,3,2,1,0:T(2,128)(2,1)}, f32[216,8,128]{2,1,0:T(8,128)}) custom-call(bf16[2,2,14,64,2,128]{5,4,3,2,1,0:T(2,128)(2,1)S(1)} %get-tuple-element.6.dg_in, f32[216,8,128]{2,1,0:T(8,128)S(1)} %get-tuple-element.7.wg_in), custom_call_target="tpu_custom_call" | custom-call | tf_op jit(solution)/shard_map/pallas_call | solution.py:388
where the time goes:
time: 42.9 us; the launch traced here: 42.8 us
  Pallas kernels  42.1 us (98%)
  between operations  0.64 us (1%)
    pallas_call x1, Pallas kernels, on_device(): pl.pallas_call(functools.partial(kernel, cfg), out_shape=(jax.ShapeDtypeS...  40.3 us
    pallas_call x1, Pallas kernels, on_device(): pl.pallas_call(store_kernel, out_shape=(jax.ShapeDtypeStruct((c_in, plane...  1.78 us

commit v1 on v0

v1 whole, which is shorter than its diff:
```python
import functools
import math

import jax
import jax.numpy as jnp
from jax import lax
from jax.experimental import pallas as pl
from jax.experimental.pallas import tpu as pltpu
from jax.sharding import PartitionSpec as P

MESH = pl.DeviceIdType.MESH
LANES = 128
UNIT = 8


def kernel(cfg, pre_hbm, cot_hbm, feat_hbm, w_hbm, dg_out, wg_out, *scr):
    (pre_v, cot_v, feat_v, w_v, m_nat, h_nat, mh, mn, feat_a, wl, wf, ws, dg_v, grad, own_a, own_b) = scr[:16]
    (r1a, r1b, r2a, r2b, r3a, r3b) = scr[16:22]
    in_sem, out_sem, halo_s, halo_r, send_sem, recv_sem = scr[22:]
    chips, chs, rows, c_in, c_out, scale, groups = cfg
    sp = lax.axis_index("sp")
    ch = lax.axis_index("ch")
    chip = sp // 2
    core = sp % 2
    flat = sp * chs + ch
    last = chips * 2 * chs - 1
    span = rows * LANES

    def chip_dev(k, c):
        return (((chip + k) % chips) * 2 + c, ch)

    def ch_dev(k):
        return (sp, (ch + k) % chs)

    bar = pltpu.get_barrier_semaphore()
    prev = jnp.maximum(flat - 1, 0)
    nxt = jnp.minimum(flat + 1, last)

    @pl.when(flat > 0)
    def _():
        pl.semaphore_signal(bar, inc=1, device_id=(prev // chs, prev % chs), device_id_type=MESH)

    @pl.when(flat < last)
    def _():
        pl.semaphore_signal(bar, inc=1, device_id=(nxt // chs, nxt % chs), device_id_type=MESH)

    loads = [
        pltpu.make_async_copy(pre_hbm.at[0], pre_v, in_sem.at[0]),
        pltpu.make_async_copy(cot_hbm.at[0], cot_v, in_sem.at[1]),
        pltpu.make_async_copy(w_hbm, w_v, in_sem.at[2]),
    ]
    loads[0].start()
    loads[1].start()
    for k in range(1, chs):
        pl.semaphore_signal(bar, inc=1, device_id=ch_dev(k), device_id_type=MESH)
    for k in range(1, chips):
        pl.semaphore_signal(bar, inc=1, device_id=chip_dev(k, core), device_id_type=MESH)
    for k in range(chips):
        pl.semaphore_signal(bar, inc=1, device_id=chip_dev(k, 1 - core), device_id_type=MESH)
    loads[2].start()

    def load_feat(k, carry):
        p, s, b = k // (2 * rows), (k // rows) % 2, k % rows
        pltpu.make_async_copy(feat_hbm.at[:, p, s, b], feat_v.at[p, s, b], in_sem.at[3]).start()
        return carry

    lax.fori_loop(0, 4 * rows, load_feat, 0)

    loads[0].wait()
    loads[1].wait()

    def mask_step(b, carry):
        p = pre_v[b].astype(jnp.float32)
        m_nat[b] = jnp.where(p > 0, cot_v[b].astype(jnp.float32), 0.0).astype(jnp.bfloat16)
        return carry

    lax.fori_loop(0, rows, mask_step, 0)
    peers = 2 * chips + chs - 2 + jnp.minimum(flat, 1) + jnp.minimum(last - flat, 1)
    pl.semaphore_wait(bar, peers)

    halo = pltpu.make_async_remote_copy(
        src_ref=m_nat, dst_ref=h_nat, send_sem=halo_s, recv_sem=halo_r,
        device_id=(prev // chs, prev % chs), device_id_type=MESH,
    )

    @pl.when(flat > 0)
    def _():
        halo.start()

    lane = lax.broadcasted_iota(jnp.int32, (c_out, LANES), 1)

    def spread(src, dst):
        dst[:, span:] = jnp.zeros((2 * c_out, LANES), jnp.bfloat16)
        for b in range(rows):
            v = src[b]
            dst[:c_out, b * LANES:(b + 1) * LANES] = v
            r = jnp.where(lane == LANES - 1, 0.0, pltpu.roll(v.astype(jnp.float32), LANES - 1, 1))
            dst[c_out:, b * LANES:(b + 1) * LANES] = r.astype(jnp.bfloat16)

    spread(m_nat, mh)
    pltpu.make_async_copy(feat_v, feat_v, in_sem.at[3]).wait()
    two = 2 * c_in

    feat_rows = feat_v.reshape(2, 2, rows, two, LANES)

    def feat_step(k, carry):
        p, s = k // 2, k % 2
        at = pl.ds(pl.multiple_of(s * two, two), two)
        for b in range(rows):
            feat_a[p, at, b * LANES:(b + 1) * LANES] = feat_rows[p, s, b]
        return carry

    lax.fori_loop(0, 4, feat_step, 0)

    ups = c_in // UNIT
    starts = {0: groups[1][0], 1: groups[0][0], 2: groups[0][0] + 9 * ups}

    def put(kd, kh, kw, val):
        base = starts[kd] + (kh * 3 + kw) * ups
        grad[base:base + ups] = val.reshape(ups, UNIT, c_out)

    def wgrad(kd, p, mm):
        dn = (((1,), (1,)), ((), ()))
        o = lax.dot_general(feat_a[p], mm[:, :span], dn, preferred_element_type=jnp.float32)
        d = lax.dot_general(feat_a[p, two:], mm[:, LANES:], dn, preferred_element_type=jnp.float32)
        for r in range(2):
            ws[r, :2 * two] = o[:, r * c_out:(r + 1) * c_out]
            ws[r, 2 * two:] = d[:, r * c_out:(r + 1) * c_out]
        for kh, part in ((1, 0), (2, 1), (0, 2)):
            for kw, r, t in ((1, 0, 0), (2, 0, 1), (0, 1, 1)):
                put(kd, kh, kw, ws[r, pl.ds(part * two + t, c_in, stride=2), :])

    def weights():
        def step(kd, carry):
            for part, kh in enumerate((1, 2, 0)):
                base = kd * 9 + kh * 3
                wf[0, pl.ds(0, c_in, stride=2), :] = w_v[base + 1].astype(jnp.float32)
                wf[0, pl.ds(1, c_in, stride=2), :] = w_v[base + 2].astype(jnp.float32)
                wf[1, pl.ds(0, c_in, stride=2), :] = jnp.zeros((c_in, c_out), jnp.float32)
                wf[1, pl.ds(1, c_in, stride=2), :] = w_v[base].astype(jnp.float32)
                for r in range(2):
                    wl[kd, part * two:(part + 1) * two, r * c_out:(r + 1) * c_out] = wf[r].astype(jnp.bfloat16)
            return carry

        lax.fori_loop(0, 3, step, 0)

    dg_rows = dg_v.reshape(2, 2, rows, two, LANES)

    def dgrad(p, terms, lo, hi):
        def step(k, carry):
            col = pl.multiple_of(k * 2 * LANES, 2 * LANES)
            here = pl.ds(col, 2 * LANES)
            down = pl.ds(pl.multiple_of(col + LANES, LANES), 2 * LANES)
            top, bot = None, None
            for kd, mm in terms:
                o = jnp.dot(wl[kd, :2 * two], mm[:, here], preferred_element_type=jnp.float32)
                d = jnp.dot(wl[kd, 2 * two:], mm[:, down], preferred_element_type=jnp.float32)
                top = o[:two] if top is None else top + o[:two]
                bot = o[two:] + d if bot is None else bot + (o[two:] + d)
            for s, val in ((0, top), (1, bot)):
                for j in range(2):
                    b = 2 * k + j
                    dg_rows[p, s, b] = val[:, j * LANES:(j + 1) * LANES].astype(jnp.bfloat16)
                    pltpu.make_async_copy(dg_v.at[p, s, b], dg_out.at[:, p, s, b], out_sem.at[0]).start()
            return carry

        lax.fori_loop(lo, hi, step, 0)

    class Reduce:
        def __init__(self, idx, r1, r2, r3, own):
            self.i, self.r1, self.r2, self.r3, self.own = idx, r1, r2, r3, own
            self.base, self.u = groups[idx]
            self.half = self.u * chips
            self.copies = {}

        def off(self, a, b):
            return self.base + a * self.half + b * self.u

        def remote(self, stage, src, dst, dev):
            return pltpu.make_async_remote_copy(
                src_ref=src, dst_ref=dst, send_sem=send_sem.at[self.i, stage - 1],
                recv_sem=recv_sem.at[self.i, stage - 1], device_id=dev, device_id_type=MESH)

        def start(self, stage):
            cps = []
            if stage == 1:
                src = grad.at[pl.ds(self.off(1 - core, 0), self.half)]
                cps.append(self.remote(1, src, self.r1, chip_dev(0, 1 - core)))
            elif stage == 2:
                for k in range(1, chips):
                    src = grad.at[pl.ds(self.off(core, (chip + k) % chips), self.u)]
                    cps.append(self.remote(2, src, self.r2.at[k - 1], chip_dev(k, core)))
            elif stage == 3:
                for k in range(1, chs):
                    cps.append(self.remote(3, self.r3.at[ch], self.r3.at[ch], ch_dev(k)))
            else:
                dst = wg_out.at[pl.ds(self.off(core, chip), self.u)]
                for k in range(1, chips):
                    cps.append(self.remote(4, self.own, dst, chip_dev(k, core)))
                for k in range(chips):
                    cps.append(self.remote(4, self.own, dst, chip_dev(k, 1 - core)))
                self.local = pltpu.make_async_copy(self.own, dst, out_sem.at[1 + self.i])
                self.local.start()
            for c in cps:
                c.start()
            self.copies[stage] = cps

        def finish(self, stage):
            if stage == 1:
                self.copies[1][0].wait()
                s = pl.ds(self.off(core, 0), self.half)
                grad[s] = grad[s] + self.r1[...]
            elif stage == 2:
                whole = pltpu.make_async_remote_copy(
                    src_ref=self.r2, dst_ref=self.r2, send_sem=send_sem.at[self.i, 1],
                    recv_sem=recv_sem.at[self.i, 1], device_id=(sp, ch), device_id_type=MESH)
                whole.wait_send()
                whole.wait_recv()
                v = grad[pl.ds(self.off(core, chip), self.u)]
                for k in range(chips - 1):
                    v = v + self.r2[k]
                self.r3[ch] = v
            elif stage == 3:
                most = self.r3.at[pl.ds(0, chs - 1)]
                whole = pltpu.make_async_remote_copy(
                    src_ref=most, dst_ref=most, send_sem=send_sem.at[self.i, 2],
                    recv_sem=recv_sem.at[self.i, 2], device_id=(sp, ch), device_id_type=MESH)
                whole.wait_send()
                whole.wait_recv()
                v = self.r3[0]
                for k in range(1, chs):
                    v = v + self.r3[k]
                self.own[...] = v * scale
            else:
                most = wg_out.at[pl.ds(self.base, (2 * chips - 1) * self.u)]
                whole = pltpu.make_async_remote_copy(
                    src_ref=most, dst_ref=most, send_sem=send_sem.at[self.i, 3],
                    recv_sem=recv_sem.at[self.i, 3], device_id=(sp, ch), device_id_type=MESH)
                whole.wait_send()
                whole.wait_recv()
                self.local.wait()

    red_a = Reduce(0, r1a, r2a, r3a, own_a)
    red_b = Reduce(1, r1b, r2b, r3b, own_b)

    for idx, taps in ((0, 18), (1, 9)):
        lo, hi = groups[idx][0] + taps * ups, groups[idx][0] + groups[idx][1] * 2 * chips
        if lo < hi:
            grad[lo:hi] = jnp.zeros((hi - lo, UNIT, LANES), jnp.float32)

    def halo_done():
        @pl.when(flat > 0)
        def _():
            halo.wait_send()

        @pl.when(flat < last)
        def _():
            halo.wait_recv()

        @pl.when(flat == last)
        def _():
            h_nat[...] = jnp.zeros_like(h_nat)

    half = rows // 2
    both = [(2, mh), (0, mn)]

    wgrad(1, 0, mh)
    wgrad(2, 1, mh)
    red_a.start(1)
    loads[2].wait()
    weights()
    red_a.finish(1)
    red_a.start(2)
    dgrad(0, [(1, mh)], 0, half)
    halo_done()
    spread(h_nat, mn)
    wgrad(0, 1, mn)
    red_b.start(1)
    red_a.finish(2)
    red_a.start(3)
    red_b.finish(1)
    red_b.start(2)
    dgrad(1, both, 0, half)
    red_b.finish(2)
    red_b.start(3)
    red_a.finish(3)
    red_a.start(4)
    red_b.finish(3)
    red_b.start(4)
    red_a.finish(4)
    red_b.finish(4)
    pltpu.make_async_copy(dg_v, dg_v, out_sem.at[0]).wait()


def store_kernel(groups, ups, dg_in, wg_in, dg_out, wg_out, sem):
    copies = [
        pltpu.make_async_copy(dg_in, dg_out, sem.at[0]),
        pltpu.make_async_copy(wg_in.at[pl.ds(groups[1][0], 9 * ups)], wg_out.at[pl.ds(0, 9 * ups)], sem.at[1]),
        pltpu.make_async_copy(wg_in.at[pl.ds(groups[0][0], 18 * ups)], wg_out.at[pl.ds(9 * ups, 18 * ups)], sem.at[2]),
    ]
    for c in copies:
        c.start()
    for c in copies:
        c.wait()


def on_device(features, pre_act, cotangent, weight):
    c_in, planes_in, _, _, rows, cols = features.shape
    c_out, planes = pre_act.shape[:2]
    taps = weight.shape[0]
    chips = lax.axis_size("sp") // 2
    chs = lax.axis_size("ch")
    devices = chips * 2 * chs
    scale = 1.0 / math.sqrt(devices * planes * rows * cols)
    ups = c_in // UNIT
    u_a = -(-18 * ups // (2 * chips))
    u_b = -(-9 * ups // (2 * chips))
    groups = ((u_b * 2 * chips, u_a), (0, u_b))
    units = (u_a + u_b) * 2 * chips
    cfg = (chips, chs, rows, c_in, c_out, scale, groups)
    bf, f32 = jnp.bfloat16, jnp.float32
    span = rows * cols
    any_spec = pl.BlockSpec(memory_space=pl.ANY)

    def part(*lead):
        return pltpu.VMEM(lead + (UNIT, c_out), f32)

    held = 2 * units + (u_a + u_b) * (2 * chips + chs)
    vmem = 17 * 2**20 + held * UNIT * c_out * 4
    dg, wg = pl.pallas_call(
        functools.partial(kernel, cfg),
        out_shape=(
            jax.ShapeDtypeStruct((c_in, 2, 2, rows, 2, cols), bf),
            jax.ShapeDtypeStruct((units, UNIT, c_out), f32),
        ),
        in_specs=[pl.BlockSpec(memory_space=pltpu.HBM)] * 4,
        out_specs=(any_spec, any_spec),
        scratch_shapes=[
            pltpu.VMEM((rows, c_out, cols), bf),
            pltpu.VMEM((rows, c_out, cols), bf),
            pltpu.VMEM((2, 2, rows, c_in, 2, cols), bf),
            pltpu.VMEM(weight.shape, bf),
            pltpu.VMEM((rows, c_out, cols), bf),
            pltpu.VMEM((rows, c_out, cols), bf),
            pltpu.VMEM((2 * c_out, span + cols), bf),
            pltpu.VMEM((2 * c_out, span + cols), bf),
            pltpu.VMEM((2, 4 * c_in, span), bf),
            pltpu.VMEM((3, 6 * c_in, 2 * c_out), bf),
            pltpu.VMEM((2, 2 * c_in, c_out), f32),
            pltpu.VMEM((2, 6 * c_in, c_out), f32),
            pltpu.VMEM((2, 2, rows, c_in, 2, cols), bf),
            part(units),
            part(u_a),
            part(u_b),
            part(u_a * chips),
            part(u_b * chips),
            part(chips - 1, u_a),
            part(chips - 1, u_b),
            part(chs, u_a),
            part(chs, u_b),
            pltpu.SemaphoreType.DMA((4,)),
            pltpu.SemaphoreType.DMA((3,)),
            pltpu.SemaphoreType.DMA,
            pltpu.SemaphoreType.DMA,
            pltpu.SemaphoreType.DMA((2, 4)),
            pltpu.SemaphoreType.DMA((2, 4)),
        ],
        compiler_params=pltpu.CompilerParams(
            collective_id=0, has_side_effects=True, vmem_limit_bytes=vmem
        ),
    )(
        pltpu.with_memory_space_constraint(pre_act.transpose(1, 2, 0, 3), pltpu.HBM),
        pltpu.with_memory_space_constraint(cotangent.transpose(1, 2, 0, 3), pltpu.HBM),
        pltpu.with_memory_space_constraint(features.transpose(0, 1, 2, 4, 3, 5), pltpu.HBM),
        pltpu.with_memory_space_constraint(weight, pltpu.HBM),
    )
    dg, wg = pl.pallas_call(
        functools.partial(store_kernel, groups, ups),
        out_shape=(
            jax.ShapeDtypeStruct((c_in, planes_in, 2, rows, 2, cols), bf),
            jax.ShapeDtypeStruct((taps * ups, UNIT, c_out), f32),
        ),
        in_specs=[any_spec] * 2,
        out_specs=(pl.BlockSpec(memory_space=pltpu.HBM),) * 2,
        scratch_shapes=[pltpu.SemaphoreType.DMA((3,))],
        compiler_params=pltpu.CompilerParams(vmem_limit_bytes=2**20),
    )(dg, wg)
    return dg.transpose(0, 1, 2, 4, 3, 5), wg.reshape(taps, c_in, c_out)


def solution(mesh):
    return jax.shard_map(
        on_device,
        mesh=mesh,
        in_specs=(
            P(None, ("sp", "ch"), None, None, None, None),
            P(None, ("sp", "ch"), None, None),
            P(None, ("sp", "ch"), None, None),
            P(),
        ),
        out_specs=(P(None, ("sp", "ch"), None, None, None, None), P()),
        check_vma=False,
    )
```

time: 42.9 us -> 37.4 us (0.87)
  Pallas kernels: 42.1 us -> 36.5 us
    pallas_call x1, Pallas kernels: 40.3 us -> 34.9 us  [on_device(): pl.pallas_call(functools.partial(kernel, cfg), out_shape=(jax.ShapeDtypeS...]
where the time goes in v1:
time: 37.4 us; the launch traced here: 37.1 us
  Pallas kernels  36.5 us (98%)
  between operations  0.64 us (2%)
    pallas_call x1, Pallas kernels, on_device(): pl.pallas_call(functools.partial(kernel, cfg), out_shape=(jax.ShapeDtypeS...  34.9 us
    pallas_call x1, Pallas kernels, on_device(): pl.pallas_call(functools.partial(store_kernel, groups, ups), out_shape=(j...  1.54 us

profile of v1, /device:TPU:0, one launch (start us, length us, event | category | flops | bytes accessed | tf_op | source)
XLA Modules:
  0.0 37.1 jit_solution(10032680973960658137)
XLA Ops:
  0.6 34.9 %shard_map.59 = (bf16[64,2,2,14,2,128]{5,4,3,2,1,0:T(2,128)(2,1)S(1)}, f32[216,8,128]{2,1,0:T(8,128)S(1)}) custom-call(bf16[1,14,128,128]{3,2,1,0:T(8,128)(2,1)} %bitcast.6, bf16[1,14,128,128]{3,2,1,0:T(8,128)(2,1)} %bitcast.7, bf16[64,2,2,14,2,128]{5,4,3,2,1,0:T(2,128)(2,1)} %bitcast.5, bf16[27,64,128]{2,1,0:T(8,128)(2,1)} %w_hbm.1), custom_call_target="tpu_custom_call" | custom-call | tf_op jit(solution)/shard_map/pallas_call | solution.py:330
  35.6 1.5 %shard_map.60 = (bf16[64,2,2,14,2,128]{5,4,3,2,1,0:T(2,128)(2,1)}, f32[216,8,128]{2,1,0:T(8,128)}) custom-call(bf16[64,2,2,14,2,128]{5,4,3,2,1,0:T(2,128)(2,1)S(1)} %get-tuple-element.6.dg_in, f32[216,8,128]{2,1,0:T(8,128)S(1)} %get-tuple-element.7.wg_in), custom_call_target="tpu_custom_call" | custom-call | tf_op jit(solution)/shard_map/pallas_call | solution.py:377

commit v2 on v1

--- a/solution.py
+++ b/solution.py
@@ -15,8 +15,8 @@
 
 def kernel(cfg, pre_hbm, cot_hbm, feat_hbm, w_hbm, dg_out, wg_out, *scr):
     (pre_v, cot_v, feat_v, w_v, m_nat, h_nat, mh, mn, feat_a, wl, wf, ws, dg_v, grad, own_a, own_b) = scr[:16]
-    (r1a, r1b, r2a, r2b, r3a, r3b) = scr[16:22]
-    in_sem, out_sem, halo_s, halo_r, send_sem, recv_sem = scr[22:]
+    (r1a, r1b, r2a, r2b, mid_a, r3a, r3b) = scr[16:23]
+    in_sem, out_sem, halo_s, halo_r, send_sem, recv_sem = scr[23:]
     chips, chs, rows, c_in, c_out, scale, groups = cfg
     sp = lax.axis_index("sp")
     ch = lax.axis_index("ch")
@@ -167,8 +167,8 @@
         lax.fori_loop(lo, hi, step, 0)
 
     class Reduce:
-        def __init__(self, idx, r1, r2, r3, own):
-            self.i, self.r1, self.r2, self.r3, self.own = idx, r1, r2, r3, own
+        def __init__(self, idx, r1, r2, r3, own, mid=None):
+            self.i, self.r1, self.r2, self.r3, self.own, self.mid = idx, r1, r2, r3, own, mid
             self.base, self.u = groups[idx]
             self.half = self.u * chips
             self.copies = {}
@@ -192,14 +192,23 @@
                     cps.append(self.remote(2, src, self.r2.at[k - 1], chip_dev(k, core)))
             elif stage == 3:
                 for k in range(1, chs):
-                    cps.append(self.remote(3, self.r3.at[ch], self.r3.at[ch], ch_dev(k)))
+                    if self.mid is None:
+                        src, dst = self.r3.at[ch], self.r3.at[ch]
+                    else:
+                        src, dst = self.mid.at[(ch + k) % chs], self.r3.at[k - 1]
+                    cps.append(self.remote(3, src, dst, ch_dev(k)))
+            elif stage == 5:
+                for k in range(1, chs):
+                    cps.append(self.remote(5, self.own.at[ch], self.own.at[ch], ch_dev(k)))
             else:
-                dst = wg_out.at[pl.ds(self.off(core, chip), self.u)]
+                own, dst = self.own, wg_out.at[pl.ds(self.off(core, chip), self.u)]
+                if self.mid is not None:
+                    own = own.reshape(self.u, UNIT, c_out)
                 for k in range(1, chips):
-                    cps.append(self.remote(4, self.own, dst, chip_dev(k, core)))
+                    cps.append(self.remote(4, own, dst, chip_dev(k, core)))
                 for k in range(chips):
-                    cps.append(self.remote(4, self.own, dst, chip_dev(k, 1 - core)))
-                self.local = pltpu.make_async_copy(self.own, dst, out_sem.at[1 + self.i])
+                    cps.append(self.remote(4, own, dst, chip_dev(k, 1 - core)))
+                self.local = pltpu.make_async_copy(own, dst, out_sem.at[1 + self.i])
                 self.local.start()
             for c in cps:
                 c.start()
@@ -219,7 +228,10 @@
                 v = grad[pl.ds(self.off(core, chip), self.u)]
                 for k in range(chips - 1):
                     v = v + self.r2[k]
-                self.r3[ch] = v
+                if self.mid is None:
+                    self.r3[ch] = v
+                else:
+                    self.mid[...] = v.reshape(self.mid.shape)
             elif stage == 3:
                 most = self.r3.at[pl.ds(0, chs - 1)]
                 whole = pltpu.make_async_remote_copy(
@@ -227,10 +239,23 @@
                     recv_sem=recv_sem.at[self.i, 2], device_id=(sp, ch), device_id_type=MESH)
                 whole.wait_send()
                 whole.wait_recv()
-                v = self.r3[0]
-                for k in range(1, chs):
-                    v = v + self.r3[k]
-                self.own[...] = v * scale
+                if self.mid is None:
+                    v = self.r3[0]
+                    for k in range(1, chs):
+                        v = v + self.r3[k]
+                    self.own[...] = (v * scale).astype(self.own.dtype)
+                else:
+                    v = self.mid[ch]
+                    for k in range(chs - 1):
+                        v = v + self.r3[k]
+                    self.own[ch] = (v * scale).astype(self.own.dtype)
+            elif stage == 5:
+                most = self.own.at[pl.ds(0, chs - 1)]
+                whole = pltpu.make_async_remote_copy(
+                    src_ref=most, dst_ref=most, send_sem=send_sem.at[self.i, 4],
+                    recv_sem=recv_sem.at[self.i, 4], device_id=(sp, ch), device_id_type=MESH)
+                whole.wait_send()
+                whole.wait_recv()
             else:
                 most = wg_out.at[pl.ds(self.base, (2 * chips - 1) * self.u)]
                 whole = pltpu.make_async_remote_copy(
@@ -240,7 +265,7 @@
                 whole.wait_recv()
                 self.local.wait()
 
-    red_a = Reduce(0, r1a, r2a, r3a, own_a)
+    red_a = Reduce(0, r1a, r2a, r3a, own_a, mid_a)
     red_b = Reduce(1, r1b, r2b, r3b, own_b)
 
     for idx, taps in ((0, 18), (1, 9)):
@@ -278,12 +303,16 @@
     red_b.start(1)
     red_a.finish(2)
     red_a.start(3)
+    dgrad(1, both, 0, 1)
     red_b.finish(1)
     red_b.start(2)
-    dgrad(1, both, 0, half)
+    dgrad(1, both, 1, 5)
+    red_a.finish(3)
+    red_a.start(5)
     red_b.finish(2)
     red_b.start(3)
-    red_a.finish(3)
+    dgrad(1, both, 5, half)
+    red_a.finish(5)
     red_a.start(4)
     red_b.finish(3)
     red_b.start(4)
@@ -292,15 +321,20 @@
     pltpu.make_async_copy(dg_v, dg_v, out_sem.at[0]).wait()
 
 
-def store_kernel(groups, ups, dg_in, wg_in, dg_out, wg_out, sem):
-    copies = [
-        pltpu.make_async_copy(dg_in, dg_out, sem.at[0]),
-        pltpu.make_async_copy(wg_in.at[pl.ds(groups[1][0], 9 * ups)], wg_out.at[pl.ds(0, 9 * ups)], sem.at[1]),
-        pltpu.make_async_copy(wg_in.at[pl.ds(groups[0][0], 18 * ups)], wg_out.at[pl.ds(9 * ups, 18 * ups)], sem.at[2]),
-    ]
-    for c in copies:
-        c.start()
-    for c in copies:
+def store_kernel(groups, ups, dg_in, wg_in, dg_out, wg_out, half_v, wide_v, sem):
+    dg_copy = pltpu.make_async_copy(dg_in, dg_out, sem.at[0])
+    dg_copy.start()
+    load = pltpu.make_async_copy(wg_in, half_v, sem.at[1])
+    load.start()
+    load.wait()
+    outs = []
+    for idx, tap0, taps in ((1, 0, 9), (0, 9, 18)):
+        here = pl.ds(tap0 * ups, taps * ups)
+        wide_v[here] = half_v[pl.ds(groups[idx][0], taps * ups)].astype(jnp.float32)
+        outs.append(pltpu.make_async_copy(wide_v.at[here], wg_out.at[here], sem.at[2 + idx]))
+        outs[-1].start()
+    dg_copy.wait()
+    for c in outs:
         c.wait()
 
 
@@ -313,7 +347,7 @@
     devices = chips * 2 * chs
     scale = 1.0 / math.sqrt(devices * planes * rows * cols)
     ups = c_in // UNIT
-    u_a = -(-18 * ups // (2 * chips))
+    u_a = -(-18 * ups // (2 * chips * chs)) * chs
     u_b = -(-9 * ups // (2 * chips))
     groups = ((u_b * 2 * chips, u_a), (0, u_b))
     units = (u_a + u_b) * 2 * chips
@@ -322,8 +356,8 @@
     span = rows * cols
     any_spec = pl.BlockSpec(memory_space=pl.ANY)
 
-    def part(*lead):
-        return pltpu.VMEM(lead + (UNIT, c_out), f32)
+    def part(*lead, dtype=f32):
+        return pltpu.VMEM(lead + (UNIT, c_out), dtype)
 
     held = 2 * units + (u_a + u_b) * (2 * chips + chs)
     vmem = 17 * 2**20 + held * UNIT * c_out * 4
@@ -331,7 +365,7 @@
         functools.partial(kernel, cfg),
         out_shape=(
             jax.ShapeDtypeStruct((c_in, 2, 2, rows, 2, cols), bf),
-            jax.ShapeDtypeStruct((units, UNIT, c_out), f32),
+            jax.ShapeDtypeStruct((units, UNIT, c_out), bf),
         ),
         in_specs=[pl.BlockSpec(memory_space=pltpu.HBM)] * 4,
         out_specs=(any_spec, any_spec),
@@ -350,20 +384,21 @@
             pltpu.VMEM((2, 6 * c_in, c_out), f32),
             pltpu.VMEM((2, 2, rows, c_in, 2, cols), bf),
             part(units),
-            part(u_a),
-            part(u_b),
+            part(chs, u_a // chs, dtype=bf),
+            part(u_b, dtype=bf),
             part(u_a * chips),
             part(u_b * chips),
             part(chips - 1, u_a),
             part(chips - 1, u_b),
-            part(chs, u_a),
+            part(chs, u_a // chs),
+            part(chs - 1, u_a // chs),
             part(chs, u_b),
             pltpu.SemaphoreType.DMA((4,)),
             pltpu.SemaphoreType.DMA((3,)),
             pltpu.SemaphoreType.DMA,
             pltpu.SemaphoreType.DMA,
-            pltpu.SemaphoreType.DMA((2, 4)),
-            pltpu.SemaphoreType.DMA((2, 4)),
+            pltpu.SemaphoreType.DMA((2, 5)),
+            pltpu.SemaphoreType.DMA((2, 5)),
         ],
         compiler_params=pltpu.CompilerParams(
             collective_id=0, has_side_effects=True, vmem_limit_bytes=vmem
@@ -382,8 +417,12 @@
         ),
         in_specs=[any_spec] * 2,
         out_specs=(pl.BlockSpec(memory_space=pltpu.HBM),) * 2,
-        scratch_shapes=[pltpu.SemaphoreType.DMA((3,))],
-        compiler_params=pltpu.CompilerParams(vmem_limit_bytes=2**20),
+        scratch_shapes=[
+            part(units, dtype=bf),
+            part(taps * ups),
+            pltpu.SemaphoreType.DMA((4,)),
+        ],
+        compiler_params=pltpu.CompilerParams(vmem_limit_bytes=2**20 + (units + 2 * taps * ups) * UNIT * c_out * 2),
     )(dg, wg)
     return dg.transpose(0, 1, 2, 4, 3, 5), wg.reshape(taps, c_in, c_out)
 

time: 37.4 us -> 34.8 us (0.930)
  Pallas kernels: 36.5 us -> 34 us
    pallas_call x1, Pallas kernels: 34.9 us -> 32.5 us  [on_device(): pl.pallas_call(functools.partial(kernel, cfg), out_shape=(jax.ShapeDtypeS...]
where the time goes in v2:
time: 34.8 us; the launch traced here: 34.7 us
  Pallas kernels  34 us (98%)
  between operations  0.64 us (2%)
    pallas_call x1, Pallas kernels, on_device(): pl.pallas_call(functools.partial(kernel, cfg), out_shape=(jax.ShapeDtypeS...  32.5 us
    pallas_call x1, Pallas kernels, on_device(): pl.pallas_call(functools.partial(store_kernel, groups, ups), out_shape=(j...  1.55 us

profile of v2, /device:TPU:0, one launch (start us, length us, event | category | flops | bytes accessed | tf_op | source)
XLA Modules:
  0.0 34.7 jit_solution(5401343111456709130)
XLA Ops:
  0.6 32.5 %shard_map.59 = (bf16[64,2,2,14,2,128]{5,4,3,2,1,0:T(2,128)(2,1)S(1)}, bf16[232,8,128]{2,1,0:T(8,128)(2,1)S(1)}) custom-call(bf16[1,14,128,128]{3,2,1,0:T(8,128)(2,1)} %bitcast.6, bf16[1,14,128,128]{3,2,1,0:T(8,128)(2,1)} %bitcast.7, bf16[64,2,2,14,2,128]{5,4,3,2,1,0:T(2,128)(2,1)} %bitcast.5, bf16[27,64,128]{2,1,0:T(8,128)(2,1)} %w_hbm.1), custom_call_target="tpu_custom_call" | custom-call | tf_op jit(solution)/shard_map/pallas_call | solution.py:364
  33.1 1.6 %shard_map.60 = (bf16[64,2,2,14,2,128]{5,4,3,2,1,0:T(2,128)(2,1)}, f32[216,8,128]{2,1,0:T(8,128)}) custom-call(bf16[64,2,2,14,2,128]{5,4,3,2,1,0:T(2,128)(2,1)S(1)} %get-tuple-element.6.dg_in, bf16[232,8,128]{2,1,0:T(8,128)(2,1)S(1)} %get-tuple-element.7.wg_in), custom_call_target="tpu_custom_call" | custom-call | tf_op jit(solution)/shard_map/pallas_call | solution.py:412

commit v3 on v2

--- a/solution.py
+++ b/solution.py
@@ -14,10 +14,10 @@
 
 
 def kernel(cfg, pre_hbm, cot_hbm, feat_hbm, w_hbm, dg_out, wg_out, *scr):
-    (pre_v, cot_v, feat_v, w_v, m_nat, h_nat, mh, mn, feat_a, wl, wf, ws, dg_v, grad, own_a, own_b) = scr[:16]
-    (r1a, r1b, r2a, r2b, mid_a, r3a, r3b) = scr[16:23]
-    in_sem, out_sem, halo_s, halo_r, send_sem, recv_sem = scr[23:]
-    chips, chs, rows, c_in, c_out, scale, groups = cfg
+    (pre_v, cot_v, feat_v, w_v, m_nat, h_nat, mh, mn, feat_a, wl, wf, ws, dg_v, grad, own_a, own_b, own_c) = scr[:17]
+    (r1a, r1d, r2a, r2d, r2b, r2c, mid_a, r3a, r3b, r3c) = scr[17:27]
+    in_sem, out_sem, halo_s, halo_r, send_sem, recv_sem = scr[27:]
+    chips, chs, rows, c_in, c_out, scale, groups, parts, sub = cfg
     sp = lax.axis_index("sp")
     ch = lax.axis_index("ch")
     chip = sp // 2
@@ -78,14 +78,20 @@
     peers = 2 * chips + chs - 2 + jnp.minimum(flat, 1) + jnp.minimum(last - flat, 1)
     pl.semaphore_wait(bar, peers)
 
-    halo = pltpu.make_async_remote_copy(
-        src_ref=m_nat, dst_ref=h_nat, send_sem=halo_s, recv_sem=halo_r,
-        device_id=(prev // chs, prev % chs), device_id_type=MESH,
-    )
+    hc = c_out // 2
+    halos = [
+        pltpu.make_async_remote_copy(
+            src_ref=m_nat.at[:, pl.ds(h * hc, hc)], dst_ref=h_nat.at[:, pl.ds(h * hc, hc)],
+            send_sem=halo_s.at[h], recv_sem=halo_r.at[h],
+            device_id=(prev // chs, prev % chs), device_id_type=MESH,
+        )
+        for h in range(2)
+    ]
 
     @pl.when(flat > 0)
     def _():
-        halo.start()
+        halos[0].start()
+        halos[1].start()
 
     lane = lax.broadcasted_iota(jnp.int32, (c_out, LANES), 1)
 
@@ -97,6 +103,15 @@
             r = jnp.where(lane == LANES - 1, 0.0, pltpu.roll(v.astype(jnp.float32), LANES - 1, 1))
             dst[c_out:, b * LANES:(b + 1) * LANES] = r.astype(jnp.bfloat16)
 
+    def spread_half(h):
+        top, low = 2 * h * hc, (2 * h + 1) * hc
+        mn[top:top + c_out, span:] = jnp.zeros((c_out, LANES), jnp.bfloat16)
+        for b in range(rows):
+            v = h_nat[b, h * hc:(h + 1) * hc]
+            mn[top:low, b * LANES:(b + 1) * LANES] = v
+            r = jnp.where(lane[:hc] == LANES - 1, 0.0, pltpu.roll(v.astype(jnp.float32), LANES - 1, 1))
+            mn[low:low + hc, b * LANES:(b + 1) * LANES] = r.astype(jnp.bfloat16)
+
     spread(m_nat, mh)
     pltpu.make_async_copy(feat_v, feat_v, in_sem.at[3]).wait()
     two = 2 * c_in
@@ -113,7 +128,7 @@
     lax.fori_loop(0, 4, feat_step, 0)
 
     ups = c_in // UNIT
-    starts = {0: groups[1][0], 1: groups[0][0], 2: groups[0][0] + 9 * ups}
+    starts = {1: parts[0], 2: parts[1]}
 
     def put(kd, kh, kw, val):
         base = starts[kd] + (kh * 3 + kw) * ups
@@ -130,6 +145,20 @@
             for kw, r, t in ((1, 0, 0), (2, 0, 1), (0, 1, 1)):
                 put(kd, kh, kw, ws[r, pl.ds(part * two + t, c_in, stride=2), :])
 
+    left = lax.broadcasted_iota(jnp.int32, (c_in, c_out), 1) < hc
+
+    def wgrad_half(h):
+        dn = (((1,), (1,)), ((), ()))
+        at = pl.ds(2 * h * hc, c_out)
+        ws[0, :2 * two] = lax.dot_general(feat_a[1], mn[at, :span], dn, preferred_element_type=jnp.float32)
+        ws[0, 2 * two:] = lax.dot_general(feat_a[1, two:], mn[at, LANES:], dn, preferred_element_type=jnp.float32)
+        even = [ws[0, pl.ds(q * two, c_in, stride=2), :] for q in range(3)]
+        odd = [ws[0, pl.ds(q * two + 1, c_in, stride=2), :] for q in range(3)]
+        packed = jnp.where(left, even[0], pltpu.roll(even[1], hc, 1))
+        for q, val in enumerate(odd + [packed, even[2]]):
+            base = groups[1 + h][0] + q * ups
+            grad[base:base + ups] = val.reshape(ups, UNIT, c_out)
+
     def weights():
         def step(kd, carry):
             for part, kh in enumerate((1, 2, 0)):
@@ -138,11 +167,18 @@
                 wf[0, pl.ds(1, c_in, stride=2), :] = w_v[base + 2].astype(jnp.float32)
                 wf[1, pl.ds(0, c_in, stride=2), :] = jnp.zeros((c_in, c_out), jnp.float32)
                 wf[1, pl.ds(1, c_in, stride=2), :] = w_v[base].astype(jnp.float32)
-                for r in range(2):
-                    wl[kd, part * two:(part + 1) * two, r * c_out:(r + 1) * c_out] = wf[r].astype(jnp.bfloat16)
+                a, z = wf[0], wf[1]
+                if swap:
+                    a, z = jnp.where(wide, a, pltpu.roll(z, hc, 1)), jnp.where(wide, pltpu.roll(a, hc, 1), z)
+                wl[kd, part * two:(part + 1) * two, :c_out] = a.astype(jnp.bfloat16)
+                wl[kd, part * two:(part + 1) * two, c_out:] = z.astype(jnp.bfloat16)
             return carry
 
-        lax.fori_loop(0, 3, step, 0)
+        wide = lax.broadcasted_iota(jnp.int32, (two, c_out), 1) < hc
+        swap = True
+        step(0, 0)
+        swap = False
+        lax.fori_loop(1, 3, step, 0)
 
     dg_rows = dg_v.reshape(2, 2, rows, two, LANES)
 
@@ -166,6 +202,46 @@
 
         lax.fori_loop(lo, hi, step, 0)
 
+    class Early:
+        def __init__(self, i, r1, r2):
+            self.i, self.r1, self.r2 = i, r1, r2
+
+        def off(self, a, k):
+            return parts[self.i] + (a * chips + k) * sub
+
+        def start(self, stage):
+            cps = []
+            if stage == 1:
+                src = grad.at[pl.ds(self.off(1 - core, 0), sub * chips)]
+                cps.append(self.remote(1, src, self.r1, chip_dev(0, 1 - core)))
+            else:
+                for k in range(1, chips):
+                    src = grad.at[pl.ds(self.off(core, (chip + k) % chips), sub)]
+                    cps.append(self.remote(2, src, self.r2.at[k - 1], chip_dev(k, core)))
+            for c in cps:
+                c.start()
+
+        def remote(self, stage, src, dst, dev):
+            at = (0, stage - 1 + 6 * self.i) if self.i == 0 else (3, stage - 1)
+            return pltpu.make_async_remote_copy(
+                src_ref=src, dst_ref=dst, send_sem=send_sem.at[at], recv_sem=recv_sem.at[at],
+                device_id=dev, device_id_type=MESH)
+
+        def finish(self, stage):
+            buf = self.r1 if stage == 1 else self.r2
+            whole = self.remote(stage, buf, buf, (sp, ch))
+            whole.wait_send()
+            whole.wait_recv()
+            if stage == 1:
+                s = pl.ds(self.off(core, 0), sub * chips)
+                grad[s] = grad[s] + self.r1[...]
+            else:
+                v = grad[pl.ds(self.off(core, chip), sub)]
+                for k in range(chips - 1):
+                    v = v + self.r2[k]
+                flat_mid = mid_a.reshape(groups[0][1], UNIT, c_out)
+                flat_mid[self.i * sub:(self.i + 1) * sub] = v
+
     class Reduce:
         def __init__(self, idx, r1, r2, r3, own, mid=None):
             self.i, self.r1, self.r2, self.r3, self.own, self.mid = idx, r1, r2, r3, own, mid
@@ -186,6 +262,11 @@
             if stage == 1:
                 src = grad.at[pl.ds(self.off(1 - core, 0), self.half)]
                 cps.append(self.remote(1, src, self.r1, chip_dev(0, 1 - core)))
+            elif stage == 2 and self.r1 is None:
+                for j in range(1, 2 * chips):
+                    k, c = j // 2, core if j % 2 == 0 else 1 - core
+                    src = grad.at[pl.ds(self.off(c, (chip + k) % chips), self.u)]
+                    cps.append(self.remote(2, src, self.r2.at[j - 1], chip_dev(k, c)))
             elif stage == 2:
                 for k in range(1, chips):
                     src = grad.at[pl.ds(self.off(core, (chip + k) % chips), self.u)]
@@ -197,6 +278,9 @@
                     else:
                         src, dst = self.mid.at[(ch + k) % chs], self.r3.at[k - 1]
                     cps.append(self.remote(3, src, dst, ch_dev(k)))
+            elif stage == 6:
+                ref = wg_out.at[pl.ds(self.off(core, 0), self.half)]
+                cps.append(self.remote(6, ref, ref, chip_dev(0, 1 - core)))
             elif stage == 5:
                 for k in range(1, chs):
                     cps.append(self.remote(5, self.own.at[ch], self.own.at[ch], ch_dev(k)))
@@ -206,7 +290,7 @@
                     own = own.reshape(self.u, UNIT, c_out)
                 for k in range(1, chips):
                     cps.append(self.remote(4, own, dst, chip_dev(k, core)))
-                for k in range(chips):
+                for k in range(chips if self.r1 is None else 0):
                     cps.append(self.remote(4, own, dst, chip_dev(k, 1 - core)))
                 self.local = pltpu.make_async_copy(own, dst, out_sem.at[1 + self.i])
                 self.local.start()
@@ -226,7 +310,7 @@
                 whole.wait_send()
                 whole.wait_recv()
                 v = grad[pl.ds(self.off(core, chip), self.u)]
-                for k in range(chips - 1):
+                for k in range(self.r2.shape[0]):
                     v = v + self.r2[k]
                 if self.mid is None:
                     self.r3[ch] = v
@@ -256,8 +340,11 @@
                     recv_sem=recv_sem.at[self.i, 4], device_id=(sp, ch), device_id_type=MESH)
                 whole.wait_send()
                 whole.wait_recv()
+            elif stage == 6:
+                self.copies[6][0].wait()
             else:
-                most = wg_out.at[pl.ds(self.base, (2 * chips - 1) * self.u)]
+                others = 2 * chips - 1 if self.r1 is None else chips - 1
+                most = wg_out.at[pl.ds(self.base, others * self.u)]
                 whole = pltpu.make_async_remote_copy(
                     src_ref=most, dst_ref=most, send_sem=send_sem.at[self.i, 3],
                     recv_sem=recv_sem.at[self.i, 3], device_id=(sp, ch), device_id_type=MESH)
@@ -265,74 +352,123 @@
                 whole.wait_recv()
                 self.local.wait()
 
-    red_a = Reduce(0, r1a, r2a, r3a, own_a, mid_a)
-    red_b = Reduce(1, r1b, r2b, r3b, own_b)
-
-    for idx, taps in ((0, 18), (1, 9)):
-        lo, hi = groups[idx][0] + taps * ups, groups[idx][0] + groups[idx][1] * 2 * chips
-        if lo < hi:
-            grad[lo:hi] = jnp.zeros((hi - lo, UNIT, LANES), jnp.float32)
-
-    def halo_done():
+    red_a = Reduce(0, r1a, None, r3a, own_a, mid_a)
+    early = [Early(0, r1a, r2a), Early(1, r1d, r2d)]
+    red_b = Reduce(1, None, r2b, r3b, own_b)
+    red_c = Reduce(2, None, r2c, r3c, own_c)
+
+    for lo, count, room in (
+        (parts[0], 9 * ups, sub * 2 * chips),
+        (parts[1], 9 * ups, sub * 2 * chips),
+        (groups[1][0], 5 * ups, groups[1][1] * 2 * chips),
+        (groups[2][0], 5 * ups, groups[2][1] * 2 * chips),
+    ):
+        if count < room:
+            grad[lo + count:lo + room] = jnp.zeros((room - count, UNIT, LANES), jnp.float32)
+    if 2 * sub < groups[0][1]:
+        rest = mid_a.reshape(groups[0][1], UNIT, c_out)
+        rest[2 * sub:] = jnp.zeros((groups[0][1] - 2 * sub, UNIT, LANES), jnp.float32)
+
+    def halo_done(h):
         @pl.when(flat > 0)
         def _():
-            halo.wait_send()
+            halos[h].wait_send()
 
         @pl.when(flat < last)
         def _():
-            halo.wait_recv()
+            halos[h].wait_recv()
 
         @pl.when(flat == last)
         def _():
-            h_nat[...] = jnp.zeros_like(h_nat)
+            h_nat[:, h * hc:(h + 1) * hc] = jnp.zeros((rows, hc, LANES), jnp.bfloat16)
 
     half = rows // 2
     both = [(2, mh), (0, mn)]
 
     wgrad(1, 0, mh)
+    early[0].start(1)
     wgrad(2, 1, mh)
-    red_a.start(1)
+    early[1].start(1)
+    early[0].finish(1)
+    early[0].start(2)
     loads[2].wait()
     weights()
-    red_a.finish(1)
-    red_a.start(2)
+    early[1].finish(1)
+    early[1].start(2)
     dgrad(0, [(1, mh)], 0, half)
-    halo_done()
-    spread(h_nat, mn)
-    wgrad(0, 1, mn)
-    red_b.start(1)
-    red_a.finish(2)
+    early[0].finish(2)
+    halo_done(0)
+    spread_half(0)
+    wgrad_half(0)
+    red_b.start(2)
+
+    early[1].finish(2)
     red_a.start(3)
-    dgrad(1, both, 0, 1)
-    red_b.finish(1)
-    red_b.start(2)
-    dgrad(1, both, 1, 5)
+    halo_done(1)
+    spread_half(1)
+    wgrad_half(1)
+    red_c.start(2)
     red_a.finish(3)
     red_a.start(5)
     red_b.finish(2)
     red_b.start(3)
-    dgrad(1, both, 5, half)
+    dgrad(1, both, 0, 4)
+    red_c.finish(2)
+    red_c.start(3)
     red_a.finish(5)
     red_a.start(4)
+    dgrad(1, both, 4, half)
     red_b.finish(3)
     red_b.start(4)
+    red_c.finish(3)
+    red_c.start(4)
     red_a.finish(4)
+    red_a.start(6)
+    red_a.finish(6)
     red_b.finish(4)
+    red_c.finish(4)
     pltpu.make_async_copy(dg_v, dg_v, out_sem.at[0]).wait()
 
 
-def store_kernel(groups, ups, dg_in, wg_in, dg_out, wg_out, half_v, wide_v, sem):
+def store_kernel(groups, sub, ups, dg_in, wg_in, dg_out, wg_out, half_v, wide_v, sem):
     dg_copy = pltpu.make_async_copy(dg_in, dg_out, sem.at[0])
     dg_copy.start()
     load = pltpu.make_async_copy(wg_in, half_v, sem.at[1])
     load.start()
     load.wait()
     outs = []
-    for idx, tap0, taps in ((1, 0, 9), (0, 9, 18)):
+
+    def send(tap0, taps, slot):
         here = pl.ds(tap0 * ups, taps * ups)
-        wide_v[here] = half_v[pl.ds(groups[idx][0], taps * ups)].astype(jnp.float32)
-        outs.append(pltpu.make_async_copy(wide_v.at[here], wg_out.at[here], sem.at[2 + idx]))
+        outs.append(pltpu.make_async_copy(wide_v.at[here], wg_out.at[here], sem.at[slot]))
         outs[-1].start()
+
+    for i in range(2):
+        for j in range(-(-9 * ups // sub)):
+            n = min(sub, 9 * ups - j * sub)
+            src = groups[0][0] + j * groups[0][1] + i * sub
+            wide_v[pl.ds(9 * (i + 1) * ups + j * sub, n)] = half_v[pl.ds(src, n)].astype(jnp.float32)
+    send(9, 18, 2)
+    lanes = half_v.shape[2]
+    left = lax.broadcasted_iota(jnp.int32, (ups * UNIT, lanes), 1) < lanes // 2
+
+    def block(h, q):
+        v = half_v[pl.ds(groups[1 + h][0] + q * ups, ups)].astype(jnp.float32)
+        return v.reshape(ups * UNIT, lanes)
+
+    def put(tap, low, high):
+        wide_v[pl.ds(tap * ups, ups)] = jnp.where(left, low, high).reshape(ups, UNIT, lanes)
+
+    def other(v):
+        return pltpu.roll(v, lanes // 2, 1)
+
+    for q, kh in enumerate((1, 2, 0)):
+        put(kh * 3 + 2, block(0, q), other(block(1, q)))
+        put(kh * 3, other(block(0, q)), block(1, q))
+    put(4, block(0, 3), other(block(1, 3)))
+    put(7, other(block(0, 3)), block(1, 3))
+    put(1, block(0, 4), other(block(1, 4)))
+    send(0, 9, 3)
     dg_copy.wait()
     for c in outs:
         c.wait()
@@ -347,11 +483,14 @@
     devices = chips * 2 * chs
     scale = 1.0 / math.sqrt(devices * planes * rows * cols)
     ups = c_in // UNIT
-    u_a = -(-18 * ups // (2 * chips * chs)) * chs
-    u_b = -(-9 * ups // (2 * chips))
-    groups = ((u_b * 2 * chips, u_a), (0, u_b))
-    units = (u_a + u_b) * 2 * chips
-    cfg = (chips, chs, rows, c_in, c_out, scale, groups)
+    sub = -(-9 * ups // (2 * chips))
+    u_a = -(-2 * sub // chs) * chs
+    u_b = -(-5 * ups // (2 * chips))
+    span_b = u_b * 2 * chips
+    groups = ((2 * span_b, u_a), (0, u_b), (span_b, u_b))
+    units = u_a * 2 * chips + 2 * span_b
+    parts = (2 * span_b, 2 * span_b + sub * 2 * chips)
+    cfg = (chips, chs, rows, c_in, c_out, scale, groups, parts, sub)
     bf, f32 = jnp.bfloat16, jnp.float32
     span = rows * cols
     any_spec = pl.BlockSpec(memory_space=pl.ANY)
@@ -359,7 +498,7 @@
     def part(*lead, dtype=f32):
         return pltpu.VMEM(lead + (UNIT, c_out), dtype)
 
-    held = 2 * units + (u_a + u_b) * (2 * chips + chs)
+    held = 2 * units + (u_a + 2 * u_b) * (2 * chips + chs)
     vmem = 17 * 2**20 + held * UNIT * c_out * 4
     dg, wg = pl.pallas_call(
         functools.partial(kernel, cfg),
@@ -386,19 +525,23 @@
             part(units),
             part(chs, u_a // chs, dtype=bf),
             part(u_b, dtype=bf),
-            part(u_a * chips),
-            part(u_b * chips),
-            part(chips - 1, u_a),
-            part(chips - 1, u_b),
+            part(u_b, dtype=bf),
+            part(sub * chips),
+            part(sub * chips),
+            part(chips - 1, sub),
+            part(chips - 1, sub),
+            part(2 * chips - 1, u_b),
+            part(2 * chips - 1, u_b),
             part(chs, u_a // chs),
             part(chs - 1, u_a // chs),
             part(chs, u_b),
+            part(chs, u_b),
             pltpu.SemaphoreType.DMA((4,)),
-            pltpu.SemaphoreType.DMA((3,)),
-            pltpu.SemaphoreType.DMA,
-            pltpu.SemaphoreType.DMA,
-            pltpu.SemaphoreType.DMA((2, 5)),
-            pltpu.SemaphoreType.DMA((2, 5)),
+            pltpu.SemaphoreType.DMA((4,)),
+            pltpu.SemaphoreType.DMA((2,)),
+            pltpu.SemaphoreType.DMA((2,)),
+            pltpu.SemaphoreType.DMA((4, 6)),
+            pltpu.SemaphoreType.DMA((4, 6)),
         ],
         compiler_params=pltpu.CompilerParams(
             collective_id=0, has_side_effects=True, vmem_limit_bytes=vmem
@@ -410,7 +553,7 @@
         pltpu.with_memory_space_constraint(weight, pltpu.HBM),
     )
     dg, wg = pl.pallas_call(
-        functools.partial(store_kernel, groups, ups),
+        functools.partial(store_kernel, groups, sub, ups),
         out_shape=(
             jax.ShapeDtypeStruct((c_in, planes_in, 2, rows, 2, cols), bf),
             jax.ShapeDtypeStruct((taps * ups, UNIT, c_out), f32),

time: 34.8 us -> 33.1 us (0.951)
  Pallas kernels: 34 us -> 32.3 us
    pallas_call x1, Pallas kernels: 32.5 us -> 30.8 us  [on_device(): pl.pallas_call(functools.partial(kernel, cfg), out_shape=(jax.ShapeDtypeS...]
where the time goes in v3:
time: 33.1 us; the launch traced here: 32.9 us
  Pallas kernels  32.3 us (98%)
  between operations  0.64 us (2%)
    pallas_call x1, Pallas kernels, on_device(): pl.pallas_call(functools.partial(kernel, cfg), out_shape=(jax.ShapeDtypeS...  30.8 us
    pallas_call x1, Pallas kernels, on_device(): pl.pallas_call(functools.partial(store_kernel, groups, sub, ups), out_sha...  1.55 us

profile of v3, /device:TPU:0, one launch (start us, length us, event | category | flops | bytes accessed | tf_op | source)
XLA Modules:
  0.0 32.9 jit_solution(8287811298503962805)
XLA Ops:
  0.6 30.8 %shard_map.59 = (bf16[64,2,2,14,2,128]{5,4,3,2,1,0:T(2,128)(2,1)S(1)}, bf16[240,8,128]{2,1,0:T(8,128)(2,1)S(1)}) custom-call(bf16[1,14,128,128]{3,2,1,0:T(8,128)(2,1)} %bitcast.6, bf16[1,14,128,128]{3,2,1,0:T(8,128)(2,1)} %bitcast.7, bf16[64,2,2,14,2,128]{5,4,3,2,1,0:T(2,128)(2,1)} %bitcast.5, bf16[27,64,128]{2,1,0:T(8,128)(2,1)} %w_hbm.1), custom_call_target="tpu_custom_call" | custom-call | tf_op jit(solution)/shard_map/pallas_call | solution.py:503
  31.4 1.5 %shard_map.60 = (bf16[64,2,2,14,2,128]{5,4,3,2,1,0:T(2,128)(2,1)}, f32[216,8,128]{2,1,0:T(8,128)}) custom-call(bf16[64,2,2,14,2,128]{5,4,3,2,1,0:T(2,128)(2,1)S(1)} %get-tuple-element.6.dg_in, bf16[240,8,128]{2,1,0:T(8,128)(2,1)S(1)} %get-tuple-element.7.wg_in), custom_call_target="tpu_custom_call" | custom-call | tf_op jit(solution)/shard_map/pallas_call | solution.py:555

commit v4 on v3

--- a/solution.py
+++ b/solution.py
@@ -16,7 +16,7 @@
 def kernel(cfg, pre_hbm, cot_hbm, feat_hbm, w_hbm, dg_out, wg_out, *scr):
     (pre_v, cot_v, feat_v, w_v, m_nat, h_nat, mh, mn, feat_a, wl, wf, ws, dg_v, grad, own_a, own_b, own_c) = scr[:17]
     (r1a, r1d, r2a, r2d, r2b, r2c, mid_a, r3a, r3b, r3c) = scr[17:27]
-    in_sem, out_sem, halo_s, halo_r, send_sem, recv_sem = scr[27:]
+    relay_v, in_sem, out_sem, halo_s, halo_r, relay_s, relay_r, send_sem, recv_sem = scr[27:]
     chips, chs, rows, c_in, c_out, scale, groups, parts, sub = cfg
     sp = lax.axis_index("sp")
     ch = lax.axis_index("ch")
@@ -88,10 +88,79 @@
         for h in range(2)
     ]
 
-    @pl.when(flat > 0)
+    wrap = jnp.logical_and(core == 0, ch == 0) if chs > 1 else False
+
+    @pl.when(jnp.logical_and(flat > 0, jnp.logical_not(wrap)))
     def _():
         halos[0].start()
         halos[1].start()
+
+    def piece(h, lo, hi):
+        return m_nat.at[pl.ds(lo, hi - lo), pl.ds(h * hc, hc)]
+
+    def landing(h, lo, hi):
+        return h_nat.at[pl.ds(lo, hi - lo), pl.ds(h * hc, hc)]
+
+    def share(c):
+        total = 1 * 2 * rows * (chips - c) // (chips * 2)
+        return min(rows, total), max(0, total - rows)
+
+    def send_wrap(c):
+        ones, zeros = share(c)
+        to, via = (2 * c - 1, chs - 1), (2 * c - 1, 0)
+        for h, lo, hi, at in (
+            (1, 0, ones, 0), (0, 0, zeros, ones), (0, zeros, rows, None), (1, ones, rows, None),
+        ):
+            if lo < hi:
+                direct = at is None
+                pltpu.make_async_remote_copy(
+                    src_ref=piece(h, lo, hi),
+                    dst_ref=landing(h, lo, hi) if direct else relay_v.at[pl.ds(at, hi - lo)],
+                    send_sem=halo_s.at[h], recv_sem=halo_r.at[h] if direct else relay_r,
+                    device_id=to if direct else via, device_id_type=MESH,
+                ).start()
+
+    for c in range(1, chips):
+        if chs > 1:
+
+            @pl.when(jnp.logical_and(wrap, chip == c))
+            def _(c=c):
+                send_wrap(c)
+
+    def forwards(c):
+        ones, zeros = share(c)
+        return [
+            pltpu.make_async_remote_copy(
+                src_ref=relay_v.at[pl.ds(at, n)], dst_ref=landing(h, 0, n),
+                send_sem=relay_s.at[h], recv_sem=halo_r.at[h],
+                device_id=(sp, chs - 1), device_id_type=MESH,
+            )
+            for h, n, at in ((1, ones, 0), (0, zeros, ones))
+            if n
+        ]
+
+    def at_relay(c):
+        return jnp.logical_and(jnp.logical_and(core == 1, ch == 0), chip == c - 1)
+
+    def relay():
+        for c in range(1, chips if chs > 1 else 1):
+            whole = relay_v.at[pl.ds(0, sum(share(c)))]
+
+            @pl.when(at_relay(c))
+            def _(c=c, whole=whole):
+                pltpu.make_async_remote_copy(
+                    src_ref=whole, dst_ref=whole, send_sem=relay_s.at[0], recv_sem=relay_r,
+                    device_id=(sp, ch), device_id_type=MESH).wait_recv()
+                for f in forwards(c):
+                    f.start()
+
+    def relay_done():
+        for c in range(1, chips if chs > 1 else 1):
+
+            @pl.when(at_relay(c))
+            def _(c=c):
+                for f in forwards(c):
+                    f.wait_send()
 
     lane = lax.broadcasted_iota(jnp.int32, (c_out, LANES), 1)
 
@@ -396,6 +465,7 @@
     early[1].finish(1)
     early[1].start(2)
     dgrad(0, [(1, mh)], 0, half)
+    relay()
     early[0].finish(2)
     halo_done(0)
     spread_half(0)
@@ -427,6 +497,7 @@
     red_a.finish(6)
     red_b.finish(4)
     red_c.finish(4)
+    relay_done()
     pltpu.make_async_copy(dg_v, dg_v, out_sem.at[0]).wait()
 
 
@@ -499,7 +570,7 @@
         return pltpu.VMEM(lead + (UNIT, c_out), dtype)
 
     held = 2 * units + (u_a + 2 * u_b) * (2 * chips + chs)
-    vmem = 17 * 2**20 + held * UNIT * c_out * 4
+    vmem = 18 * 2**20 + held * UNIT * c_out * 4
     dg, wg = pl.pallas_call(
         functools.partial(kernel, cfg),
         out_shape=(
@@ -536,10 +607,13 @@
             part(chs - 1, u_a // chs),
             part(chs, u_b),
             part(chs, u_b),
+            pltpu.VMEM((2 * rows, c_out // 2, cols), bf),
             pltpu.SemaphoreType.DMA((4,)),
             pltpu.SemaphoreType.DMA((4,)),
             pltpu.SemaphoreType.DMA((2,)),
             pltpu.SemaphoreType.DMA((2,)),
+            pltpu.SemaphoreType.DMA((2,)),
+            pltpu.SemaphoreType.DMA,
             pltpu.SemaphoreType.DMA((4, 6)),
             pltpu.SemaphoreType.DMA((4, 6)),
         ],

time: 33.1 us -> 32.7 us (0.988)
    pallas_call x1, Pallas kernels: 30.8 us -> 30.4 us  [on_device(): pl.pallas_call(functools.partial(kernel, cfg), out_shape=(jax.ShapeDtypeS...]
where the time goes in v4:
time: 32.7 us; the launch traced here: 32.6 us
  Pallas kernels  32 us (98%)
  between operations  0.64 us (2%)
    pallas_call x1, Pallas kernels, on_device(): pl.pallas_call(functools.partial(kernel, cfg), out_shape=(jax.ShapeDtypeS...  30.4 us
    pallas_call x1, Pallas kernels, on_device(): pl.pallas_call(functools.partial(store_kernel, groups, sub, ups), out_sha...  1.55 us

profile of v4, /device:TPU:0, one launch (start us, length us, event | category | flops | bytes accessed | tf_op | source)
XLA Modules:
  0.0 32.6 jit_solution(8344827430560455134)
XLA Ops:
  0.6 30.4 %shard_map.59 = (bf16[64,2,2,14,2,128]{5,4,3,2,1,0:T(2,128)(2,1)S(1)}, bf16[240,8,128]{2,1,0:T(8,128)(2,1)S(1)}) custom-call(bf16[1,14,128,128]{3,2,1,0:T(8,128)(2,1)} %bitcast.6, bf16[1,14,128,128]{3,2,1,0:T(8,128)(2,1)} %bitcast.7, bf16[64,2,2,14,2,128]{5,4,3,2,1,0:T(2,128)(2,1)} %bitcast.5, bf16[27,64,128]{2,1,0:T(8,128)(2,1)} %w_hbm.1), custom_call_target="tpu_custom_call" | custom-call | tf_op jit(solution)/shard_map/pallas_call | solution.py:574
  31.1 1.5 %shard_map.60 = (bf16[64,2,2,14,2,128]{5,4,3,2,1,0:T(2,128)(2,1)}, f32[216,8,128]{2,1,0:T(8,128)}) custom-call(bf16[64,2,2,14,2,128]{5,4,3,2,1,0:T(2,128)(2,1)S(1)} %get-tuple-element.6.dg_in, bf16[240,8,128]{2,1,0:T(8,128)(2,1)S(1)} %get-tuple-element.7.wg_in), custom_call_target="tpu_custom_call" | custom-call | tf_op jit(solution)/shard_map/pallas_call | solution.py:629

commit v5 on v4

--- a/solution.py
+++ b/solution.py
@@ -102,7 +102,7 @@
         return h_nat.at[pl.ds(lo, hi - lo), pl.ds(h * hc, hc)]
 
     def share(c):
-        total = 1 * 2 * rows * (chips - c) // (chips * 2)
+        total = 3 * 2 * rows * (chips - c) // (chips * 4)
         return min(rows, total), max(0, total - rows)
 
     def send_wrap(c):
@@ -464,8 +464,9 @@
     weights()
     early[1].finish(1)
     early[1].start(2)
-    dgrad(0, [(1, mh)], 0, half)
+    dgrad(0, [(1, mh)], 0, 3)
     relay()
+    dgrad(0, [(1, mh)], 3, half)
     early[0].finish(2)
     halo_done(0)
     spread_half(0)

time: 32.7 us -> 32.2 us (0.985)
  Pallas kernels: 32 us -> 31.4 us
    pallas_call x1, Pallas kernels: 30.4 us -> 29.8 us  [on_device(): pl.pallas_call(functools.partial(kernel, cfg), out_shape=(jax.ShapeDtypeS...]
where the time goes in v5:
time: 32.2 us; the launch traced here: 32 us
  Pallas kernels  31.4 us (98%)
  between operations  0.64 us (2%)
    pallas_call x1, Pallas kernels, on_device(): pl.pallas_call(functools.partial(kernel, cfg), out_shape=(jax.ShapeDtypeS...  29.8 us
    pallas_call x1, Pallas kernels, on_device(): pl.pallas_call(functools.partial(store_kernel, groups, sub, ups), out_sha...  1.55 us

profile of v5, /device:TPU:0, one launch (start us, length us, event | category | flops | bytes accessed | tf_op | source)
XLA Modules:
  0.0 32.0 jit_solution(11658068018217321951)
XLA Ops:
  0.6 29.8 %shard_map.59 = (bf16[64,2,2,14,2,128]{5,4,3,2,1,0:T(2,128)(2,1)S(1)}, bf16[240,8,128]{2,1,0:T(8,128)(2,1)S(1)}) custom-call(bf16[1,14,128,128]{3,2,1,0:T(8,128)(2,1)} %bitcast.6, bf16[1,14,128,128]{3,2,1,0:T(8,128)(2,1)} %bitcast.7, bf16[64,2,2,14,2,128]{5,4,3,2,1,0:T(2,128)(2,1)} %bitcast.5, bf16[27,64,128]{2,1,0:T(8,128)(2,1)} %w_hbm.1), custom_call_target="tpu_custom_call" | custom-call | tf_op jit(solution)/shard_map/pallas_call | solution.py:575
  30.5 1.5 %shard_map.60 = (bf16[64,2,2,14,2,128]{5,4,3,2,1,0:T(2,128)(2,1)}, f32[216,8,128]{2,1,0:T(8,128)}) custom-call(bf16[64,2,2,14,2,128]{5,4,3,2,1,0:T(2,128)(2,1)S(1)} %get-tuple-element.6.dg_in, bf16[240,8,128]{2,1,0:T(8,128)(2,1)S(1)} %get-tuple-element.7.wg_in), custom_call_target="tpu_custom_call" | custom-call | tf_op jit(solution)/shard_map/pallas_call | solution.py:630

commit v6 on v5

--- a/solution.py
+++ b/solution.py
@@ -49,14 +49,14 @@
         pltpu.make_async_copy(cot_hbm.at[0], cot_v, in_sem.at[1]),
         pltpu.make_async_copy(w_hbm, w_v, in_sem.at[2]),
     ]
-    loads[0].start()
-    loads[1].start()
     for k in range(1, chs):
         pl.semaphore_signal(bar, inc=1, device_id=ch_dev(k), device_id_type=MESH)
     for k in range(1, chips):
         pl.semaphore_signal(bar, inc=1, device_id=chip_dev(k, core), device_id_type=MESH)
     for k in range(chips):
         pl.semaphore_signal(bar, inc=1, device_id=chip_dev(k, 1 - core), device_id_type=MESH)
+    loads[0].start()
+    loads[1].start()
     loads[2].start()
 
     def load_feat(k, carry):
@@ -74,7 +74,7 @@
         m_nat[b] = jnp.where(p > 0, cot_v[b].astype(jnp.float32), 0.0).astype(jnp.bfloat16)
         return carry
 
-    lax.fori_loop(0, rows, mask_step, 0)
+    lax.fori_loop(0, rows, mask_step, 0, unroll=True)
     peers = 2 * chips + chs - 2 + jnp.minimum(flat, 1) + jnp.minimum(last - flat, 1)
     pl.semaphore_wait(bar, peers)
 
@@ -102,22 +102,30 @@
         return h_nat.at[pl.ds(lo, hi - lo), pl.ds(h * hc, hc)]
 
     def share(c):
-        total = 3 * 2 * rows * (chips - c) // (chips * 4)
+        total = 7 * 2 * rows * (chips - c) // (8 * chips)
         return min(rows, total), max(0, total - rows)
+
+    def legs(c, slot):
+        ones, zeros = share(c)
+        cut = (ones + zeros + 1) // 2
+        lo, hi = (0, cut) if slot == 0 else (cut, ones + zeros)
+        parts_of = ((1, lo, min(hi, ones), lo), (0, max(lo, ones) - ones, hi - ones, max(lo, ones)))
+        return lo, hi, [p for p in parts_of if p[1] < p[2]]
 
     def send_wrap(c):
         ones, zeros = share(c)
         to, via = (2 * c - 1, chs - 1), (2 * c - 1, 0)
-        for h, lo, hi, at in (
-            (1, 0, ones, 0), (0, 0, zeros, ones), (0, zeros, rows, None), (1, ones, rows, None),
-        ):
-            if lo < hi:
-                direct = at is None
+        for slot in range(2):
+            for h, lo, hi, at in legs(c, slot)[2]:
                 pltpu.make_async_remote_copy(
-                    src_ref=piece(h, lo, hi),
-                    dst_ref=landing(h, lo, hi) if direct else relay_v.at[pl.ds(at, hi - lo)],
-                    send_sem=halo_s.at[h], recv_sem=halo_r.at[h] if direct else relay_r,
-                    device_id=to if direct else via, device_id_type=MESH,
+                    src_ref=piece(h, lo, hi), dst_ref=relay_v.at[pl.ds(at, hi - lo)],
+                    send_sem=halo_s.at[h], recv_sem=relay_r.at[slot], device_id=via, device_id_type=MESH,
+                ).start()
+        for h, lo in ((0, zeros), (1, ones)):
+            if lo < rows:
+                pltpu.make_async_remote_copy(
+                    src_ref=piece(h, lo, rows), dst_ref=landing(h, lo, rows),
+                    send_sem=halo_s.at[h], recv_sem=halo_r.at[h], device_id=to, device_id_type=MESH,
                 ).start()
 
     for c in range(1, chips):
@@ -127,40 +135,44 @@
             def _(c=c):
                 send_wrap(c)
 
-    def forwards(c):
-        ones, zeros = share(c)
+    def forwards(c, slot):
         return [
             pltpu.make_async_remote_copy(
-                src_ref=relay_v.at[pl.ds(at, n)], dst_ref=landing(h, 0, n),
-                send_sem=relay_s.at[h], recv_sem=halo_r.at[h],
+                src_ref=relay_v.at[pl.ds(at, hi - lo)], dst_ref=landing(h, lo, hi),
+                send_sem=relay_s.at[slot], recv_sem=halo_r.at[h],
                 device_id=(sp, chs - 1), device_id_type=MESH,
             )
-            for h, n, at in ((1, ones, 0), (0, zeros, ones))
-            if n
+            for h, lo, hi, at in legs(c, slot)[2]
         ]
 
     def at_relay(c):
         return jnp.logical_and(jnp.logical_and(core == 1, ch == 0), chip == c - 1)
 
-    def relay():
+    def relayed(c, slot):
+        lo, hi, _ = legs(c, slot)
+        whole = relay_v.at[pl.ds(lo, hi - lo)]
+        return pltpu.make_async_remote_copy(
+            src_ref=whole, dst_ref=whole, send_sem=relay_s.at[slot], recv_sem=relay_r.at[slot],
+            device_id=(sp, ch), device_id_type=MESH)
+
+    def relay(slot):
         for c in range(1, chips if chs > 1 else 1):
-            whole = relay_v.at[pl.ds(0, sum(share(c)))]
-
-            @pl.when(at_relay(c))
-            def _(c=c, whole=whole):
-                pltpu.make_async_remote_copy(
-                    src_ref=whole, dst_ref=whole, send_sem=relay_s.at[0], recv_sem=relay_r,
-                    device_id=(sp, ch), device_id_type=MESH).wait_recv()
-                for f in forwards(c):
-                    f.start()
+            if legs(c, slot)[2]:
+
+                @pl.when(at_relay(c))
+                def _(c=c):
+                    relayed(c, slot).wait_recv()
+                    for f in forwards(c, slot):
+                        f.start()
 
     def relay_done():
         for c in range(1, chips if chs > 1 else 1):
-
-            @pl.when(at_relay(c))
-            def _(c=c):
-                for f in forwards(c):
-                    f.wait_send()
+            for slot in range(2):
+                if legs(c, slot)[2]:
+
+                    @pl.when(at_relay(c))
+                    def _(c=c, slot=slot):
+                        relayed(c, slot).wait_send()
 
     lane = lax.broadcasted_iota(jnp.int32, (c_out, LANES), 1)
 
@@ -271,6 +283,8 @@
 
         lax.fori_loop(lo, hi, step, 0)
 
+    sent = []
+
     class Early:
         def __init__(self, i, r1, r2):
             self.i, self.r1, self.r2 = i, r1, r2
@@ -299,8 +313,8 @@
         def finish(self, stage):
             buf = self.r1 if stage == 1 else self.r2
             whole = self.remote(stage, buf, buf, (sp, ch))
-            whole.wait_send()
             whole.wait_recv()
+            sent.append(whole)
             if stage == 1:
                 s = pl.ds(self.off(core, 0), sub * chips)
                 grad[s] = grad[s] + self.r1[...]
@@ -369,15 +383,16 @@
 
         def finish(self, stage):
             if stage == 1:
-                self.copies[1][0].wait()
+                self.copies[1][0].wait_recv()
+                sent.append(self.copies[1][0])
                 s = pl.ds(self.off(core, 0), self.half)
                 grad[s] = grad[s] + self.r1[...]
             elif stage == 2:
                 whole = pltpu.make_async_remote_copy(
                     src_ref=self.r2, dst_ref=self.r2, send_sem=send_sem.at[self.i, 1],
                     recv_sem=recv_sem.at[self.i, 1], device_id=(sp, ch), device_id_type=MESH)
-                whole.wait_send()
                 whole.wait_recv()
+                sent.append(whole)
                 v = grad[pl.ds(self.off(core, chip), self.u)]
                 for k in range(self.r2.shape[0]):
                     v = v + self.r2[k]
@@ -390,8 +405,8 @@
                 whole = pltpu.make_async_remote_copy(
                     src_ref=most, dst_ref=most, send_sem=send_sem.at[self.i, 2],
                     recv_sem=recv_sem.at[self.i, 2], device_id=(sp, ch), device_id_type=MESH)
-                whole.wait_send()
                 whole.wait_recv()
+                sent.append(whole)
                 if self.mid is None:
                     v = self.r3[0]
                     for k in range(1, chs):
@@ -407,18 +422,19 @@
                 whole = pltpu.make_async_remote_copy(
                     src_ref=most, dst_ref=most, send_sem=send_sem.at[self.i, 4],
                     recv_sem=recv_sem.at[self.i, 4], device_id=(sp, ch), device_id_type=MESH)
-                whole.wait_send()
                 whole.wait_recv()
+                sent.append(whole)
             elif stage == 6:
-                self.copies[6][0].wait()
+                self.copies[6][0].wait_recv()
+                sent.append(self.copies[6][0])
             else:
                 others = 2 * chips - 1 if self.r1 is None else chips - 1
                 most = wg_out.at[pl.ds(self.base, others * self.u)]
                 whole = pltpu.make_async_remote_copy(
                     src_ref=most, dst_ref=most, send_sem=send_sem.at[self.i, 3],
                     recv_sem=recv_sem.at[self.i, 3], device_id=(sp, ch), device_id_type=MESH)
-                whole.wait_send()
                 whole.wait_recv()
+                sent.append(whole)
                 self.local.wait()
 
     red_a = Reduce(0, r1a, None, r3a, own_a, mid_a)
@@ -438,11 +454,16 @@
         rest = mid_a.reshape(groups[0][1], UNIT, c_out)
         rest[2 * sub:] = jnp.zeros((groups[0][1] - 2 * sub, UNIT, LANES), jnp.float32)
 
-    def halo_done(h):
+    def all_sent():
         @pl.when(flat > 0)
         def _():
-            halos[h].wait_send()
-
+            halos[0].wait_send()
+            halos[1].wait_send()
+
+        for c in sent:
+            c.wait_send()
+
+    def halo_done(h):
         @pl.when(flat < last)
         def _():
             halos[h].wait_recv()
@@ -464,8 +485,9 @@
     weights()
     early[1].finish(1)
     early[1].start(2)
+    relay(0)
     dgrad(0, [(1, mh)], 0, 3)
-    relay()
+    relay(1)
     dgrad(0, [(1, mh)], 3, half)
     early[0].finish(2)
     halo_done(0)
@@ -499,6 +521,7 @@
     red_b.finish(4)
     red_c.finish(4)
     relay_done()
+    all_sent()
     pltpu.make_async_copy(dg_v, dg_v, out_sem.at[0]).wait()
 
 
@@ -614,7 +637,7 @@
             pltpu.SemaphoreType.DMA((2,)),
             pltpu.SemaphoreType.DMA((2,)),
             pltpu.SemaphoreType.DMA((2,)),
-            pltpu.SemaphoreType.DMA,
+            pltpu.SemaphoreType.DMA((2,)),
             pltpu.SemaphoreType.DMA((4, 6)),
             pltpu.SemaphoreType.DMA((4, 6)),
         ],

time: 32.2 us -> 32.1 us (level)
  no operation moved by 1% of the time
where the time goes in v6:
time: 32.1 us; the launch traced here: 32 us
  Pallas kernels  31.3 us (98%)
  between operations  0.64 us (2%)
    pallas_call x1, Pallas kernels, on_device(): pl.pallas_call(functools.partial(kernel, cfg), out_shape=(jax.ShapeDtypeS...  29.8 us
    pallas_call x1, Pallas kernels, on_device(): pl.pallas_call(functools.partial(store_kernel, groups, sub, ups), out_sha...  1.55 us

profile of v6, /device:TPU:0, one launch (start us, length us, event | category | flops | bytes accessed | tf_op | source)
XLA Modules:
  0.0 32.0 jit_solution(12800551071136366492)
XLA Ops:
  0.6 29.8 %shard_map.59 = (bf16[64,2,2,14,2,128]{5,4,3,2,1,0:T(2,128)(2,1)S(1)}, bf16[240,8,128]{2,1,0:T(8,128)(2,1)S(1)}) custom-call(bf16[1,14,128,128]{3,2,1,0:T(8,128)(2,1)} %bitcast.6, bf16[1,14,128,128]{3,2,1,0:T(8,128)(2,1)} %bitcast.7, bf16[64,2,2,14,2,128]{5,4,3,2,1,0:T(2,128)(2,1)} %bitcast.5, bf16[27,64,128]{2,1,0:T(8,128)(2,1)} %w_hbm.1), custom_call_target="tpu_custom_call" | custom-call | tf_op jit(solution)/shard_map/pallas_call | solution.py:598
  30.4 1.5 %shard_map.60 = (bf16[64,2,2,14,2,128]{5,4,3,2,1,0:T(2,128)(2,1)}, f32[216,8,128]{2,1,0:T(8,128)}) custom-call(bf16[64,2,2,14,2,128]{5,4,3,2,1,0:T(2,128)(2,1)S(1)} %get-tuple-element.6.dg_in, bf16[240,8,128]{2,1,0:T(8,128)(2,1)S(1)} %get-tuple-element.7.wg_in), custom_call_target="tpu_custom_call" | custom-call | tf_op jit(solution)/shard_map/pallas_call | solution.py:653

commit v7 on v6

--- a/solution.py
+++ b/solution.py
@@ -283,6 +283,9 @@
 
         lax.fori_loop(lo, hi, step, 0)
 
+    def slot(i, k):
+        return k + {0: 0, 3: 6, 1: 7, 2: 10}[i]
+
     sent = []
 
     class Early:
@@ -305,7 +308,7 @@
                 c.start()
 
         def remote(self, stage, src, dst, dev):
-            at = (0, stage - 1 + 6 * self.i) if self.i == 0 else (3, stage - 1)
+            at = slot(0 if self.i == 0 else 3, stage - 1)
             return pltpu.make_async_remote_copy(
                 src_ref=src, dst_ref=dst, send_sem=send_sem.at[at], recv_sem=recv_sem.at[at],
                 device_id=dev, device_id_type=MESH)
@@ -337,8 +340,8 @@
 
         def remote(self, stage, src, dst, dev):
             return pltpu.make_async_remote_copy(
-                src_ref=src, dst_ref=dst, send_sem=send_sem.at[self.i, stage - 1],
-                recv_sem=recv_sem.at[self.i, stage - 1], device_id=dev, device_id_type=MESH)
+                src_ref=src, dst_ref=dst, send_sem=send_sem.at[slot(self.i, stage - 1)],
+                recv_sem=recv_sem.at[slot(self.i, stage - 1)], device_id=dev, device_id_type=MESH)
 
         def start(self, stage):
             cps = []
@@ -389,8 +392,8 @@
                 grad[s] = grad[s] + self.r1[...]
             elif stage == 2:
                 whole = pltpu.make_async_remote_copy(
-                    src_ref=self.r2, dst_ref=self.r2, send_sem=send_sem.at[self.i, 1],
-                    recv_sem=recv_sem.at[self.i, 1], device_id=(sp, ch), device_id_type=MESH)
+                    src_ref=self.r2, dst_ref=self.r2, send_sem=send_sem.at[slot(self.i, 1)],
+                    recv_sem=recv_sem.at[slot(self.i, 1)], device_id=(sp, ch), device_id_type=MESH)
                 whole.wait_recv()
                 sent.append(whole)
                 v = grad[pl.ds(self.off(core, chip), self.u)]
@@ -403,8 +406,8 @@
             elif stage == 3:
                 most = self.r3.at[pl.ds(0, chs - 1)]
                 whole = pltpu.make_async_remote_copy(
-                    src_ref=most, dst_ref=most, send_sem=send_sem.at[self.i, 2],
-                    recv_sem=recv_sem.at[self.i, 2], device_id=(sp, ch), device_id_type=MESH)
+                    src_ref=most, dst_ref=most, send_sem=send_sem.at[slot(self.i, 2)],
+                    recv_sem=recv_sem.at[slot(self.i, 2)], device_id=(sp, ch), device_id_type=MESH)
                 whole.wait_recv()
                 sent.append(whole)
                 if self.mid is None:
@@ -420,8 +423,8 @@
             elif stage == 5:
                 most = self.own.at[pl.ds(0, chs - 1)]
                 whole = pltpu.make_async_remote_copy(
-                    src_ref=most, dst_ref=most, send_sem=send_sem.at[self.i, 4],
-                    recv_sem=recv_sem.at[self.i, 4], device_id=(sp, ch), device_id_type=MESH)
+                    src_ref=most, dst_ref=most, send_sem=send_sem.at[slot(self.i, 4)],
+                    recv_sem=recv_sem.at[slot(self.i, 4)], device_id=(sp, ch), device_id_type=MESH)
                 whole.wait_recv()
                 sent.append(whole)
             elif stage == 6:
@@ -431,8 +434,8 @@
                 others = 2 * chips - 1 if self.r1 is None else chips - 1
                 most = wg_out.at[pl.ds(self.base, others * self.u)]
                 whole = pltpu.make_async_remote_copy(
-                    src_ref=most, dst_ref=most, send_sem=send_sem.at[self.i, 3],
-                    recv_sem=recv_sem.at[self.i, 3], device_id=(sp, ch), device_id_type=MESH)
+                    src_ref=most, dst_ref=most, send_sem=send_sem.at[slot(self.i, 3)],
+                    recv_sem=recv_sem.at[slot(self.i, 3)], device_id=(sp, ch), device_id_type=MESH)
                 whole.wait_recv()
                 sent.append(whole)
                 self.local.wait()
@@ -638,8 +641,8 @@
             pltpu.SemaphoreType.DMA((2,)),
             pltpu.SemaphoreType.DMA((2,)),
             pltpu.SemaphoreType.DMA((2,)),
-            pltpu.SemaphoreType.DMA((4, 6)),
-            pltpu.SemaphoreType.DMA((4, 6)),
+            pltpu.SemaphoreType.DMA((14,)),
+            pltpu.SemaphoreType.DMA((14,)),
         ],
         compiler_params=pltpu.CompilerParams(
             collective_id=0, has_side_effects=True, vmem_limit_bytes=vmem

time: 32.1 us -> 32 us (level)
  no operation moved by 1% of the time
where the time goes in v7:
time: 32 us; the launch traced here: 31.8 us
  Pallas kernels  31.2 us (98%)
  between operations  0.64 us (2%)
    pallas_call x1, Pallas kernels, on_device(): pl.pallas_call(functools.partial(kernel, cfg), out_shape=(jax.ShapeDtypeS...  29.6 us
    pallas_call x1, Pallas kernels, on_device(): pl.pallas_call(functools.partial(store_kernel, groups, sub, ups), out_sha...  1.55 us

profile of v7, /device:TPU:0, one launch (start us, length us, event | category | flops | bytes accessed | tf_op | source)
XLA Modules:
  0.0 31.8 jit_solution(18309915750865453773)
XLA Ops:
  0.6 29.6 %shard_map.59 = (bf16[64,2,2,14,2,128]{5,4,3,2,1,0:T(2,128)(2,1)S(1)}, bf16[240,8,128]{2,1,0:T(8,128)(2,1)S(1)}) custom-call(bf16[1,14,128,128]{3,2,1,0:T(8,128)(2,1)} %bitcast.6, bf16[1,14,128,128]{3,2,1,0:T(8,128)(2,1)} %bitcast.7, bf16[64,2,2,14,2,128]{5,4,3,2,1,0:T(2,128)(2,1)} %bitcast.5, bf16[27,64,128]{2,1,0:T(8,128)(2,1)} %w_hbm.1), custom_call_target="tpu_custom_call" | custom-call | tf_op jit(solution)/shard_map/pallas_call | solution.py:601
  30.2 1.5 %shard_map.60 = (bf16[64,2,2,14,2,128]{5,4,3,2,1,0:T(2,128)(2,1)}, f32[216,8,128]{2,1,0:T(8,128)}) custom-call(bf16[64,2,2,14,2,128]{5,4,3,2,1,0:T(2,128)(2,1)S(1)} %get-tuple-element.6.dg_in, bf16[240,8,128]{2,1,0:T(8,128)(2,1)S(1)} %get-tuple-element.7.wg_in), custom_call_target="tpu_custom_call" | custom-call | tf_op jit(solution)/shard_map/pallas_call | solution.py:656
